TPU v7x, 512 devices: a whole 4x4x16 slice. The times are simulated.
512 devices in a mesh: row: 16 (over x, z_lo), col: 32 (over y, z_hi, core).
Axes of the slice: x: 4, y: 4, z: 16 (z_hi: 4, z_lo: 4; z = z_hi * 4 + z_lo), core: 2. Of those that a mesh axis runs over, the one named last changes fastest.
Arguments:
- probes: bfloat16 [32, 262144], P(None, ('row', 'col')), may hold values from -6 to 6
- tiles: bfloat16 [16, 32, 9, 512, 512], P('row', 'col'), may hold values from -0.09375 to 0.09375
- tile_index: int32 [16, 32, 9, 2], P('row', 'col'), may hold values from 0 to 31, as said below
- tile_count: int32 [16, 32], P('row', 'col'), may hold values from 2 to 9, as said below
- coefficients: float32 [5], replicated, may hold values from 0.2 to 1
Outputs:
- heat: float32 [32, 262144], P(None, ('row', 'col'))
Inputs may be any that keep to these rules, and one draw needn't show every extreme that they name: `tile_index`: on each device the 9 slots name distinct positions (local block row below 32, local block column below 16); slot 0 is the tile whose block row and block column are both the first block of the device's own probe segment. `tile_count`: at least one device holds exactly 9 live slots.
All inputs are finite; a program needn't handle non-finite values.
Results may differ from a plain program's by a relative error of at most 0.029.
Values may be sent and summed in bfloat16 or wider, within the bound.
No kernel may reach another device: no remote copies, remote signals or barrier semaphores. Data moves between devices by JAX's collectives and lax.ppermute only.
A program may use at most 64 MiB of HBM per device.

v0:
```python
import jax
import jax.numpy as jnp
from jax import lax
from jax.sharding import PartitionSpec as P

TILE = 512
ITERS = 4


def on_device(probes, tiles, tile_index, tile_count, coefficients):
    groups = lax.axis_size("col")
    width = probes.shape[0]
    seg_len = probes.shape[1]
    seg_blk = seg_len // TILE
    out_blocks = groups * seg_blk
    slabs = tiles[0, 0]
    where_rows = tile_index[0, 0, :, 0]
    where_cols = tile_index[0, 0, :, 1]
    in_use = (lax.iota(jnp.int32, slabs.shape[0]) < tile_count[0, 0]).astype(jnp.float32)

    def operate(field_bf):
        panel = lax.all_gather(field_bf, "row", axis=1, tiled=True)
        blocks = panel.reshape(width, -1, TILE)
        picked = jnp.take(blocks, where_cols, axis=1)
        products = jnp.einsum("ktb,tab->kta", picked, slabs, preferred_element_type=jnp.float32)
        products = products * in_use[None, :, None]
        onehot = (where_rows[:, None] == lax.iota(jnp.int32, out_blocks)[None, :]).astype(
            jnp.float32
        )
        partial_value = jnp.einsum("kta,tr->rka", products, onehot, precision=lax.Precision.HIGHEST)
        mine = lax.psum_scatter(
            partial_value.astype(jnp.bfloat16), "col", scatter_dimension=0, tiled=True
        ).astype(jnp.float32)
        return jnp.transpose(mine, (1, 0, 2)).reshape(width, seg_len)

    previous = probes.astype(jnp.float32)
    current = operate(probes)
    heat = coefficients[0] * previous + coefficients[1] * current
    for order in range(2, ITERS + 1):
        following = 2.0 * operate(current.astype(jnp.bfloat16)) - previous
        previous, current = (current, following)
        heat = heat + coefficients[order] * following
    return heat


def solution(mesh):
    return jax.shard_map(
        on_device,
        mesh=mesh,
        in_specs=(
            P(None, ("row", "col")),
            P("row", "col", None, None, None),
            P("row", "col", None, None),
            P("row", "col"),
            P(),
        ),
        out_specs=P(None, ("row", "col")),
        check_vma=False,
    )
```

profile of v0, /device:TPU:1, one launch (start us, length us, event | category | flops | bytes accessed | tf_op | source)
XLA Modules:
  0.0 666.6 jit_solution(16609068609730106789)
XLA Ops:
  6.5 0.7 compare_and_fusion
  7.9 42.2 %all_gather.12 = bf16[32,8192]{1,0:T(8,128)(2,1)S(1)} all-gather(bf16[32,512]{1,0:T(8,128)(2,1)} %param.7), channel_id=1, replica_groups=mesh['row'=16,'col'=32] {'row'}, dimensions={1}, use_global_device_ids=true | all-gather | bytes 557056 | tf_op jit(solution)/shard_map/all_gather | solution.py:22
  51.4 3.8 fusion.29
  55.2 1.3 convolution_convert_fusion.3
  56.5 1.5 copy.82
  58.1 118.4 %reduce-scatter.5.cloned.1.call-done = bf16[1,32,512]{2,1,0:T(8,128)(2,1)} async-done(((bf16[32,32,512]{2,1,0:T(8,128)(2,1)}), bf16[1,32,512]{2,1,0:T(8,128)(2,1)}) %reduce-scatter.5.cloned.1.call-update) | async-done | bytes 32784 | tf_op jit(solution)/shard_map/reduce_scatter | solution.py:31
  176.5 37.6 %all-gather = bf16[1,32,8192]{2,1,0:T(8,128)(2,1)S(1)} all-gather(bf16[1,32,512]{2,1,0:T(8,128)(2,1)} %reduce-scatter.5.cloned.1.call-done), channel_id=2, replica_groups=mesh['row'=16,'col'=32] {'row'}, dimensions={2}, use_global_device_ids=true | all-gather | bytes 557056 | tf_op jit(solution)/shard_map/all_gather | solution.py:22
  215.2 3.8 fusion.26
  219.0 1.3 convolution_convert_fusion.2
  220.2 1.5 copy.85
  221.9 113.9 %reduce-scatter.7.cloned.1.call-done = bf16[1,32,512]{2,1,0:T(8,128)(2,1)} async-done(((bf16[32,32,512]{2,1,0:T(8,128)(2,1)}), bf16[1,32,512]{2,1,0:T(8,128)(2,1)}) %reduce-scatter.7.cloned.1.call-update) | async-done | bytes 32784 | tf_op jit(solution)/shard_map/reduce_scatter | solution.py:31
  335.8 0.8 fusion.59
  336.6 37.4 %all_gather.14 = bf16[32,8192]{1,0:T(8,128)(2,1)S(1)} all-gather(bf16[32,512]{1,0:T(8,128)(2,1)S(1)} %fusion.59), channel_id=1, replica_groups=mesh['row'=16,'col'=32] {'row'}, dimensions={1}, use_global_device_ids=true | all-gather | bytes 557056 | tf_op jit(solution)/shard_map/all_gather | solution.py:22
  374.7 3.8 fusion.23
  378.5 1.3 convolution_convert_fusion.1
  379.7 1.5 copy.88
  381.4 114.0 %reduce-scatter.9.cloned.1.call-done = bf16[1,32,512]{2,1,0:T(8,128)(2,1)} async-done(((bf16[32,32,512]{2,1,0:T(8,128)(2,1)}), bf16[1,32,512]{2,1,0:T(8,128)(2,1)}) %reduce-scatter.9.cloned.1.call-update) | async-done | bytes 32784 | tf_op jit(solution)/shard_map/reduce_scatter | solution.py:31
  495.4 0.8 fusion.58
  496.1 37.3 %all-gather.1 = bf16[1,32,8192]{2,1,0:T(8,128)(2,1)S(1)} all-gather(bf16[1,32,512]{2,1,0:T(8,128)(2,1)S(1)} %fusion.58), channel_id=3, replica_groups=mesh['row'=16,'col'=32] {'row'}, dimensions={2}, use_global_device_ids=true | all-gather | bytes 557056 | tf_op jit(solution)/shard_map/all_gather | solution.py:22
  534.5 3.8 fusion.20
  538.3 1.3 convolution_convert_fusion
  539.6 1.5 copy.91
  541.9 113.6 %reduce-scatter.11.cloned.1.call-done = bf16[1,32,512]{2,1,0:T(8,128)(2,1)} async-done(((bf16[32,32,512]{2,1,0:T(8,128)(2,1)}), bf16[1,32,512]{2,1,0:T(8,128)(2,1)}) %reduce-scatter.11.cloned.1.call-update) | async-done | bytes 32784 | tf_op jit(solution)/shard_map/reduce_scatter | solution.py:31
  655.5 4.6 fusion.55
  (32 shorter events, 4.8 us)
Async XLA Ops:
  6.5 170.0 %reduce-scatter.5.cloned.1.call-start = ((), (), s32[]{:S(2)}) async-start(), calls=%async_computation.4 | async-start | bytes 1081344 | tf_op jit(solution)/shard_map/reduce_scatter | solution.py:31
  58.1 277.8 %reduce-scatter.7.cloned.1.call-start = ((), (), s32[]{:S(2)}) async-start(), calls=%async_computation.5 | async-start | bytes 1081344 | tf_op jit(solution)/shard_map/reduce_scatter | solution.py:31
  215.1 120.7 %copy-start = (bf16[32,512]{1,0:T(8,128)(2,1)S(1)}, bf16[32,512]{1,0:T(8,128)(2,1)}, u32[]{:S(2)}) copy-start(bf16[32,512]{1,0:T(8,128)(2,1)} %param.7) | copy-start | bytes 98308
  221.8 273.5 %reduce-scatter.9.cloned.1.call-start = ((), (), s32[]{:S(2)}) async-start(), calls=%async_computation.6 | async-start | bytes 1081344 | tf_op jit(solution)/shard_map/reduce_scatter | solution.py:31
  374.6 120.7 %copy-start.1 = (bf16[1,32,512]{2,1,0:T(8,128)(2,1)S(1)}, bf16[1,32,512]{2,1,0:T(8,128)(2,1)}, u32[]{:S(2)}) copy-start(bf16[1,32,512]{2,1,0:T(8,128)(2,1)} %reduce-scatter.5.cloned.1.call-done) | copy-start | bytes 98308
  381.3 274.2 %reduce-scatter.11.cloned.1.call-start = ((), (), s32[]{:S(2)}) async-start(), calls=%async_computation.7 | async-start | bytes 1081344 | tf_op jit(solution)/shard_map/reduce_scatter | solution.py:31
  534.5 6.7 %copy-start.4 = (f32[5]{0:T(128)S(1)}, f32[5]{0:T(128)}, u32[]{:S(2)}) copy-start(f32[5]{0:T(128)} %param.11) | copy-start | bytes 64
  534.5 121.0 %copy-start.2 = (bf16[1,32,512]{2,1,0:T(8,128)(2,1)S(1)}, bf16[1,32,512]{2,1,0:T(8,128)(2,1)}, u32[]{:S(2)}) copy-start(bf16[1,32,512]{2,1,0:T(8,128)(2,1)} %reduce-scatter.7.cloned.1.call-done) | copy-start | bytes 98308
  534.5 121.0 %copy-start.3 = (bf16[1,32,512]{2,1,0:T(8,128)(2,1)S(1)}, bf16[1,32,512]{2,1,0:T(8,128)(2,1)}, u32[]{:S(2)}) copy-start(bf16[1,32,512]{2,1,0:T(8,128)(2,1)} %reduce-scatter.9.cloned.1.call-done) | copy-start | bytes 98308
Sparse Core Ops, SparseCore 0:
  58.2 118.2 reduce-scatter.4
  221.9 113.8 reduce-scatter.6
  381.4 113.8 reduce-scatter.8
  541.3 114.1 reduce-scatter.10
where the time goes:
time: 668 us; the launch traced here: 667 us
  waiting for transfers between devices  460 us (69%)
  blocking collectives  155 us (23%)
  matrix products  20.3 us (3%)
  between operations  13.9 us (2%)
  local copies, waits for them, and re-layouts  10.8 us (2%)
  other arithmetic  6.85 us (1%)
    reduce_scatter x4, waiting for transfers between devices, operate(): lax.psum_scatter(partial_value.astype(jnp.bfloat16), 'col', scatter_dimen...  460 us
    all_gather x4, blocking collectives, operate(): panel = lax.all_gather(field_bf, 'row', axis=1, tiled=True)  155 us
    dot_general x4, matrix products, operate(): jnp.einsum('ktb,tab->kta', picked, slabs, preferred_element_type=jnp.floa...  15.3 us
  transfers between devices with their start and end apart: 4, of which 4 were waited for; matrix products, arithmetic and copies ran while one was open for 0% of the time, Pallas kernels for 0%

commit v1 on v0

v1 whole, which is shorter than its diff:
```python
import jax
import jax.numpy as jnp
from jax import lax
from jax.experimental import pallas as pl
from jax.experimental.pallas import tpu as pltpu
from jax.sharding import Mesh, PartitionSpec as P

TILE = 512
ITERS = 4
AXES = ("x", "zl", "y", "zh", "c")
SIZES = (4, 4, 4, 4, 2)


def tile_kernel(index_ref, count_ref, core_ref, panel_ref, tiles_ref, mine_ref, theirs_ref, acc_ref):
    acc_ref[...] = jnp.zeros_like(acc_ref)
    count = count_ref[0]
    core = core_ref[0]
    for slot in range(tiles_ref.shape[0]):
        row = index_ref[2 * slot]
        col = index_ref[2 * slot + 1]
        picked = panel_ref[col]
        picked = jnp.where(slot < count, picked, jnp.zeros_like(picked))
        product = lax.dot_general(
            picked, tiles_ref[slot], (((1,), (1,)), ((), ())), preferred_element_type=jnp.float32
        )
        away = (row % 2) ^ core
        at = away * 16 + row // 2
        acc_ref[at] += product
    mine_ref[...] = acc_ref[:16].astype(jnp.bfloat16)
    theirs_ref[...] = acc_ref[16:].astype(jnp.bfloat16)


def on_device(probes, tiles, tile_index, tile_count, coefficients):
    width = probes.shape[0]
    slabs = tiles[0, 0]
    index = tile_index[0, 0].reshape(-1)
    count = tile_count[0]
    core = lax.axis_index("c").astype(jnp.int32).reshape(1)
    smem = pl.BlockSpec(memory_space=pltpu.SMEM)
    vmem = pl.BlockSpec(memory_space=pltpu.VMEM)
    half = jax.ShapeDtypeStruct((16, width, TILE), jnp.bfloat16)
    multiply = pl.pallas_call(
        tile_kernel,
        out_shape=(half, half),
        in_specs=[smem, smem, smem, vmem, vmem],
        out_specs=(vmem, vmem),
        scratch_shapes=[pltpu.VMEM((32, width, TILE), jnp.float32)],
        compiler_params=pltpu.CompilerParams(vmem_limit_bytes=32 * 1024 * 1024),
        name="tiles",
    )

    def spread(field, axis):
        copies = jnp.broadcast_to(field[None], (4,) + field.shape)
        return lax.all_to_all(copies, axis, 0, 0, tiled=True)

    def total(parts, axis):
        arrived = lax.all_to_all(parts, axis, 0, 0, tiled=True)
        return jnp.sum(arrived.astype(jnp.float32), axis=0)

    def operate(field_bf):
        panel = spread(spread(field_bf, "zl"), "x").reshape(16, width, TILE)
        mine, theirs = multiply(index, count, core, panel, slabs)
        other = lax.ppermute(theirs, "c", [(0, 1), (1, 0)])
        chip = (mine.astype(jnp.float32) + other.astype(jnp.float32)).astype(jnp.bfloat16)
        along_y = total(chip.reshape(4, 4, width, TILE), "y").astype(jnp.bfloat16)
        return total(along_y, "zh")

    previous = probes.astype(jnp.float32)
    current = operate(probes)
    heat = coefficients[0] * previous + coefficients[1] * current
    for order in range(2, ITERS + 1):
        following = 2.0 * operate(current.astype(jnp.bfloat16)) - previous
        previous, current = (current, following)
        heat = heat + coefficients[order] * following
    return heat


def solution(mesh):
    physical = Mesh(mesh.devices.reshape(SIZES), AXES)
    row, col = AXES[:2], AXES[2:]
    return jax.shard_map(
        on_device,
        mesh=physical,
        in_specs=(
            P(None, AXES),
            P(row, col, None, None, None),
            P(row, col, None, None),
            P(row, col),
            P(),
        ),
        out_specs=P(None, AXES),
        check_vma=False,
    )
```

time: 668 us -> 256 us (0.38)
  waiting for transfers between devices: 460 us -> 23.2 us
  starting transfers between devices: 0.13 us -> 39.9 us
  matrix products: 20.3 us -> 0 us
  between operations: 13.9 us -> 0.9 us
  Pallas kernels: 0 us -> 8.16 us
  blocking collectives: 155 us -> 162 us
    reduce_scatter x4 -> x0, waiting for transfers between devices: 460 us -> none  [operate(): lax.psum_scatter(partial_value.astype(jnp.bfloat16), 'col', scatter_dimen...]
    all_to_all x0 -> x14, blocking collectives: none -> 162 us  [the longest x7 100 us: total(): arrived = lax.all_to_all(parts, axis, 0, 0, tiled=True)]
    all_gather x4 -> x0, blocking collectives: 155 us -> none  [operate(): panel = lax.all_gather(field_bf, 'row', axis=1, tiled=True)]
    ppermute x0 -> x4, starting transfers between devices: none -> 32.6 us  [operate(): other = lax.ppermute(theirs, 'c', [(0, 1), (1, 0)])]
    dot_general x8 -> x0, matrix products: 20.3 us -> none  [the longest x4 15.3 us: operate(): jnp.einsum('ktb,tab->kta', picked, slabs, preferred_element_type=jnp.floa...]
    all_to_all x0 -> x2, waiting for transfers between devices: none -> 17.2 us  [the longest x1 11.8 us: total(): arrived = lax.all_to_all(parts, axis, 0, 0, tiled=True)]
    unnamed x12 -> x13, local copies, waits for them, and re-layouts: 0.35 us -> 10.1 us
    pallas_call x0 -> x4, Pallas kernels: none -> 8.16 us  [operate(): mine, theirs = multiply(index, count, core, panel, slabs)]
  transfers between devices with their start and end apart: 4 -> 6, of which waited for: 4 -> 6; matrix products, arithmetic and copies ran while one was open for 0% -> 1% of each run, Pallas kernels for 0% -> 0%
where the time goes in v1:
time: 256 us; the launch traced here: 252 us
  blocking collectives  162 us (63%)
  starting transfers between devices  39.9 us (16%)
  waiting for transfers between devices  23.2 us (9%)
  local copies, waits for them, and re-layouts  12.6 us (5%)
  Pallas kernels  8.16 us (3%)
  other arithmetic  5.47 us (2%)
    all_to_all x7, blocking collectives, total(): arrived = lax.all_to_all(parts, axis, 0, 0, tiled=True)  100 us
    all_to_all x7, blocking collectives, spread(): return lax.all_to_all(copies, axis, 0, 0, tiled=True)  62.1 us
    ppermute x4, starting transfers between devices, operate(): other = lax.ppermute(theirs, 'c', [(0, 1), (1, 0)])  32.6 us
    all_to_all x1, waiting for transfers between devices, total(): arrived = lax.all_to_all(parts, axis, 0, 0, tiled=True)  11.8 us
    unnamed x13, local copies, waits for them, and re-layouts  10.1 us
    pallas_call x4, Pallas kernels, operate(): mine, theirs = multiply(index, count, core, panel, slabs)  8.16 us
    ppermute x4, waiting for transfers between devices, operate(): other = lax.ppermute(theirs, 'c', [(0, 1), (1, 0)])  6.06 us
    all_to_all x1, waiting for transfers between devices, spread(): return lax.all_to_all(copies, axis, 0, 0, tiled=True)  5.43 us
  transfers between devices with their start and end apart: 6, of which 6 were waited for; matrix products, arithmetic and copies ran while one was open for 1% of the time, Pallas kernels for 0%

profile of v1, /device:TPU:1, one launch (start us, length us, event | category | flops | bytes accessed | tf_op | source)
XLA Modules:
  0.0 252.5 jit_solution(8034498540475764183)
XLA Ops:
  0.8 11.0 %all_to_all.80 = bf16[4,32,512]{2,1,0:T(8,128)(2,1)S(1)} all-to-all(bf16[4,32,512]{2,1,0:T(8,128)(2,1)S(1)} %broadcast_in_dim.16), channel_id=1, replica_groups=mesh['x'=4,'zl'=4,'y'=4,'zh'=4,'c'=2] {'zl'}, dimensions={0} | all-to-all | bytes 262144 | tf_op jit(solution)/shard_map/all_to_all | solution.py:54
  12.6 4.1 %all-to-all-start.1 = ((bf16[4,4,32,512]{3,2,1,0:T(8,128)(2,1)}), bf16[4,4,32,512]{3,2,1,0:T(8,128)(2,1)S(1)}, u32[]{:S(2)}, u32[]{:S(2)}) async-start(bf16[4,4,32,512]{3,2,1,0:T(8,128)(2,1)} %broadcast_in_dim.17), calls=%async_computation.1 | async-start | bytes 1048576 | tf_op jit(solution)/shard_map/all_to_all | solution.py:54
  18.2 5.4 %all-to-all-done.1 = bf16[4,4,32,512]{3,2,1,0:T(8,128)(2,1)S(1)} async-done(((bf16[4,4,32,512]{3,2,1,0:T(8,128)(2,1)}), bf16[4,4,32,512]{3,2,1,0:T(8,128)(2,1)S(1)}, u32[]{:S(2)}, u32[]{:S(2)}) %all-to-all-start.1) | async-done | bytes 524320 | tf_op jit(solution)/shard_map/all_to_all | solution.py:54
  23.6 2.3 copy-done
  28.0 6.6 %collective-permute-start = (bf16[16,32,512]{2,1,0:T(8,128)(2,1)S(1)}, bf16[16,32,512]{2,1,0:T(8,128)(2,1)S(1)}, u32[]{:S(2)}, u32[]{:S(2)}) collective-permute-start(bf16[16,32,512]{2,1,0:T(8,128)(2,1)S(1)} %get-tuple-element.14), channel_id=1, source_target_pairs={{0,1},{1,0},{2,3},{3,2},{4,5},{5,4},{6,7},{7,6},{8,9},{9,8},{10,11... | collective-permute-start | bytes 1572872 | tf_op jit(solution)/shard_map/ppermute | solution.py:63
  36.3 11.5 %all_to_all.81 = bf16[4,4,32,512]{3,2,1,0:T(8,128)(2,1)S(1)} all-to-all(bf16[4,4,32,512]{3,2,1,0:T(8,128)(2,1)S(1)} %bitcast.28), channel_id=1, replica_groups=mesh['x'=4,'zl'=4,'y'=4,'zh'=4,'c'=2] {'y'}, dimensions={0} | all-to-all | bytes 1048576 | tf_op jit(solution)/shard_map/all_to_all | solution.py:57
  47.9 24.0 %all_to_all.82 = bf16[4,32,512]{2,1,0:T(8,128)(2,1)S(1)} all-to-all(bf16[4,32,512]{2,1,0:T(8,128)(2,1)S(1)} %reduce_sum.84), channel_id=1, replica_groups=mesh['x'=4,'zl'=4,'y'=4,'zh'=4,'c'=2] {'zh'}, dimensions={0} | all-to-all | bytes 262144 | tf_op jit(solution)/shard_map/all_to_all | solution.py:57
  72.0 7.8 %all_to_all.83 = bf16[4,32,512]{2,1,0:T(8,128)(2,1)S(1)} all-to-all(bf16[4,32,512]{2,1,0:T(8,128)(2,1)S(1)} %broadcast_in_dim.18), channel_id=1, replica_groups=mesh['x'=4,'zl'=4,'y'=4,'zh'=4,'c'=2] {'zl'}, dimensions={0} | all-to-all | bytes 262144 | tf_op jit(solution)/shard_map/all_to_all | solution.py:54
  79.8 9.3 %all_to_all.84 = bf16[4,4,32,512]{3,2,1,0:T(8,128)(2,1)S(1)} all-to-all(bf16[4,4,32,512]{3,2,1,0:T(8,128)(2,1)S(1)} %broadcast_in_dim.19), channel_id=1, replica_groups=mesh['x'=4,'zl'=4,'y'=4,'zh'=4,'c'=2] {'x'}, dimensions={0} | all-to-all | bytes 1048576 | tf_op jit(solution)/shard_map/all_to_all | solution.py:54
  93.5 9.1 %collective-permute-start.1 = (bf16[16,32,512]{2,1,0:T(8,128)(2,1)S(1)}, bf16[16,32,512]{2,1,0:T(8,128)(2,1)S(1)}, u32[]{:S(2)}, u32[]{:S(2)}) collective-permute-start(bf16[16,32,512]{2,1,0:T(8,128)(2,1)S(1)} %get-tuple-element.16), channel_id=1, source_target_pairs={{0,1},{1,0},{2,3},{3,2},{4,5},{5,4},{6,7},{7,6},{8,9},{9,8},{10,11... | collective-permute-start | bytes 1572872 | tf_op jit(solution)/shard_map/ppermute | solution.py:63
  104.3 11.6 %all_to_all.85 = bf16[4,4,32,512]{3,2,1,0:T(8,128)(2,1)S(1)} all-to-all(bf16[4,4,32,512]{3,2,1,0:T(8,128)(2,1)S(1)} %bitcast.29), channel_id=1, replica_groups=mesh['x'=4,'zl'=4,'y'=4,'zh'=4,'c'=2] {'y'}, dimensions={0} | all-to-all | bytes 1048576 | tf_op jit(solution)/shard_map/all_to_all | solution.py:57
  116.0 14.9 %all_to_all.86 = bf16[4,32,512]{2,1,0:T(8,128)(2,1)S(1)} all-to-all(bf16[4,32,512]{2,1,0:T(8,128)(2,1)S(1)} %reduce_sum.86), channel_id=1, replica_groups=mesh['x'=4,'zl'=4,'y'=4,'zh'=4,'c'=2] {'zh'}, dimensions={0} | all-to-all | bytes 262144 | tf_op jit(solution)/shard_map/all_to_all | solution.py:57
  130.9 8.0 %all_to_all.87 = bf16[4,32,512]{2,1,0:T(8,128)(2,1)S(1)} all-to-all(bf16[4,32,512]{2,1,0:T(8,128)(2,1)S(1)} %broadcast_in_dim.20), channel_id=1, replica_groups=mesh['x'=4,'zl'=4,'y'=4,'zh'=4,'c'=2] {'zl'}, dimensions={0} | all-to-all | bytes 262144 | tf_op jit(solution)/shard_map/all_to_all | solution.py:54
  138.9 9.3 %all_to_all.88 = bf16[4,4,32,512]{3,2,1,0:T(8,128)(2,1)S(1)} all-to-all(bf16[4,4,32,512]{3,2,1,0:T(8,128)(2,1)S(1)} %broadcast_in_dim.21), channel_id=1, replica_groups=mesh['x'=4,'zl'=4,'y'=4,'zh'=4,'c'=2] {'x'}, dimensions={0} | all-to-all | bytes 1048576 | tf_op jit(solution)/shard_map/all_to_all | solution.py:54
  152.7 8.1 %collective-permute-start.2 = (bf16[16,32,512]{2,1,0:T(8,128)(2,1)S(1)}, bf16[16,32,512]{2,1,0:T(8,128)(2,1)S(1)}, u32[]{:S(2)}, u32[]{:S(2)}) collective-permute-start(bf16[16,32,512]{2,1,0:T(8,128)(2,1)S(1)} %get-tuple-element.18), channel_id=1, source_target_pairs={{0,1},{1,0},{2,3},{3,2},{4,5},{5,4},{6,7},{7,6},{8,9},{9,8},{10,11... | collective-permute-start | bytes 1572872 | tf_op jit(solution)/shard_map/ppermute | solution.py:63
  162.4 11.6 %all_to_all.89 = bf16[4,4,32,512]{3,2,1,0:T(8,128)(2,1)S(1)} all-to-all(bf16[4,4,32,512]{3,2,1,0:T(8,128)(2,1)S(1)} %bitcast.30), channel_id=1, replica_groups=mesh['x'=4,'zl'=4,'y'=4,'zh'=4,'c'=2] {'y'}, dimensions={0} | all-to-all | bytes 1048576 | tf_op jit(solution)/shard_map/all_to_all | solution.py:57
  174.1 14.7 %all_to_all.90 = bf16[4,32,512]{2,1,0:T(8,128)(2,1)S(1)} all-to-all(bf16[4,32,512]{2,1,0:T(8,128)(2,1)S(1)} %reduce_sum.88), channel_id=1, replica_groups=mesh['x'=4,'zl'=4,'y'=4,'zh'=4,'c'=2] {'zh'}, dimensions={0} | all-to-all | bytes 262144 | tf_op jit(solution)/shard_map/all_to_all | solution.py:57
  188.9 7.4 %all_to_all.91 = bf16[4,32,512]{2,1,0:T(8,128)(2,1)S(1)} all-to-all(bf16[4,32,512]{2,1,0:T(8,128)(2,1)S(1)} %broadcast_in_dim.22), channel_id=1, replica_groups=mesh['x'=4,'zl'=4,'y'=4,'zh'=4,'c'=2] {'zl'}, dimensions={0} | all-to-all | bytes 262144 | tf_op jit(solution)/shard_map/all_to_all | solution.py:54
  196.3 9.3 %all_to_all.92 = bf16[4,4,32,512]{3,2,1,0:T(8,128)(2,1)S(1)} all-to-all(bf16[4,4,32,512]{3,2,1,0:T(8,128)(2,1)S(1)} %broadcast_in_dim.23), channel_id=1, replica_groups=mesh['x'=4,'zl'=4,'y'=4,'zh'=4,'c'=2] {'x'}, dimensions={0} | all-to-all | bytes 1048576 | tf_op jit(solution)/shard_map/all_to_all | solution.py:54
  210.1 8.8 %collective-permute-start.3 = (bf16[16,32,512]{2,1,0:T(8,128)(2,1)S(1)}, bf16[16,32,512]{2,1,0:T(8,128)(2,1)S(1)}, u32[]{:S(2)}, u32[]{:S(2)}) collective-permute-start(bf16[16,32,512]{2,1,0:T(8,128)(2,1)S(1)} %get-tuple-element.20), channel_id=1, source_target_pairs={{0,1},{1,0},{2,3},{3,2},{4,5},{5,4},{6,7},{7,6},{8,9},{9,8},{10,11... | collective-permute-start | bytes 1572872 | tf_op jit(solution)/shard_map/ppermute | solution.py:63
  220.6 11.6 %all_to_all.93 = bf16[4,4,32,512]{3,2,1,0:T(8,128)(2,1)S(1)} all-to-all(bf16[4,4,32,512]{3,2,1,0:T(8,128)(2,1)S(1)} %bitcast.31), channel_id=1, replica_groups=mesh['x'=4,'zl'=4,'y'=4,'zh'=4,'c'=2] {'y'}, dimensions={0} | all-to-all | bytes 1048576 | tf_op jit(solution)/shard_map/all_to_all | solution.py:57
  232.9 3.3 %all-to-all-start.15 = ((bf16[4,32,512]{2,1,0:T(8,128)(2,1)}), bf16[4,32,512]{2,1,0:T(8,128)(2,1)S(1)}, u32[]{:S(2)}, u32[]{:S(2)}) async-start(bf16[4,32,512]{2,1,0:T(8,128)(2,1)} %reduce_sum.90), calls=%async_computation.15 | async-start | bytes 262144 | tf_op jit(solution)/shard_map/all_to_all | solution.py:57
  236.9 11.8 %all-to-all-done.15 = bf16[4,32,512]{2,1,0:T(8,128)(2,1)S(1)} async-done(((bf16[4,32,512]{2,1,0:T(8,128)(2,1)}), bf16[4,32,512]{2,1,0:T(8,128)(2,1)S(1)}, u32[]{:S(2)}, u32[]{:S(2)}) %all-to-all-start.15) | async-done | bytes 131104 | tf_op jit(solution)/shard_map/all_to_all | solution.py:57
  248.7 3.8 %fusion.3 = f32[32,512]{1,0:T(8,128)} fusion(bf16[32,512]{1,0:T(8,128)(2,1)S(1)} %copy-done.4, f32[32,512]{1,0:T(8,128)S(1)} %convert_reduce_fusion, f32[32,512]{1,0:T(8,128)S(1)} %convert_reduce_fusion.3, f32[32,512]{1,0:T(8,128)S(1)} %convert_reduce_fusion.2, f32[]{:T(128)} %bitcast.13, f32[]{:T(128)} %bitcast.10, f32[32,512]{1,0:T(8,128)S(1)} %convert_reduce_fusion.1, ...), kind=kLoop, calls=%fused_computation.13 | loop fusion | flops 262144 | bytes 360468 | tf_op jit(solution)/shard_map/add | solution.py:74
  (45 shorter events, 26.2 us)
Async XLA Ops:
  12.6 11.0 %all-to-all-start.1 = ((bf16[4,4,32,512]{3,2,1,0:T(8,128)(2,1)}), bf16[4,4,32,512]{3,2,1,0:T(8,128)(2,1)S(1)}, u32[]{:S(2)}, u32[]{:S(2)}) async-start(bf16[4,4,32,512]{3,2,1,0:T(8,128)(2,1)} %broadcast_in_dim.17), calls=%async_computation.1 | async-start | bytes 1048576 | tf_op jit(solution)/shard_map/all_to_all | solution.py:54
  23.6 2.3 copy-start
  28.0 8.1 %collective-permute-start = (bf16[16,32,512]{2,1,0:T(8,128)(2,1)S(1)}, bf16[16,32,512]{2,1,0:T(8,128)(2,1)S(1)}, u32[]{:S(2)}, u32[]{:S(2)}) collective-permute-start(bf16[16,32,512]{2,1,0:T(8,128)(2,1)S(1)} %get-tuple-element.14), channel_id=1, source_target_pairs={{0,1},{1,0},{2,3},{3,2},{4,5},{5,4},{6,7},{7,6},{8,9},{9,8},{10,11... | collective-permute-start | bytes 1572872 | tf_op jit(solution)/shard_map/ppermute | solution.py:63
  79.8 51.1 %copy-start.4 = (bf16[32,512]{1,0:T(8,128)(2,1)S(1)}, bf16[32,512]{1,0:T(8,128)(2,1)}, u32[]{:S(2)}) copy-start(bf16[32,512]{1,0:T(8,128)(2,1)} %param.5) | copy-start | bytes 98308
  89.2 2.3 copy-start.1
  93.5 10.6 %collective-permute-start.1 = (bf16[16,32,512]{2,1,0:T(8,128)(2,1)S(1)}, bf16[16,32,512]{2,1,0:T(8,128)(2,1)S(1)}, u32[]{:S(2)}, u32[]{:S(2)}) collective-permute-start(bf16[16,32,512]{2,1,0:T(8,128)(2,1)S(1)} %get-tuple-element.16), channel_id=1, source_target_pairs={{0,1},{1,0},{2,3},{3,2},{4,5},{5,4},{6,7},{7,6},{8,9},{9,8},{10,11... | collective-permute-start | bytes 1572872 | tf_op jit(solution)/shard_map/ppermute | solution.py:63
  148.3 2.3 copy-start.2
  152.7 9.6 %collective-permute-start.2 = (bf16[16,32,512]{2,1,0:T(8,128)(2,1)S(1)}, bf16[16,32,512]{2,1,0:T(8,128)(2,1)S(1)}, u32[]{:S(2)}, u32[]{:S(2)}) collective-permute-start(bf16[16,32,512]{2,1,0:T(8,128)(2,1)S(1)} %get-tuple-element.18), channel_id=1, source_target_pairs={{0,1},{1,0},{2,3},{3,2},{4,5},{5,4},{6,7},{7,6},{8,9},{9,8},{10,11... | collective-permute-start | bytes 1572872 | tf_op jit(solution)/shard_map/ppermute | solution.py:63
  196.3 39.9 %copy-start.5 = (f32[5]{0:T(128)S(1)}, f32[5]{0:T(128)}, u32[]{:S(2)}) copy-start(f32[5]{0:T(128)} %param.9) | copy-start | bytes 64
  205.7 2.3 copy-start.3
  210.1 10.4 %collective-permute-start.3 = (bf16[16,32,512]{2,1,0:T(8,128)(2,1)S(1)}, bf16[16,32,512]{2,1,0:T(8,128)(2,1)S(1)}, u32[]{:S(2)}, u32[]{:S(2)}) collective-permute-start(bf16[16,32,512]{2,1,0:T(8,128)(2,1)S(1)} %get-tuple-element.20), channel_id=1, source_target_pairs={{0,1},{1,0},{2,3},{3,2},{4,5},{5,4},{6,7},{7,6},{8,9},{9,8},{10,11... | collective-permute-start | bytes 1572872 | tf_op jit(solution)/shard_map/ppermute | solution.py:63
  232.9 15.8 %all-to-all-start.15 = ((bf16[4,32,512]{2,1,0:T(8,128)(2,1)}), bf16[4,32,512]{2,1,0:T(8,128)(2,1)S(1)}, u32[]{:S(2)}, u32[]{:S(2)}) async-start(bf16[4,32,512]{2,1,0:T(8,128)(2,1)} %reduce_sum.90), calls=%async_computation.15 | async-start | bytes 262144 | tf_op jit(solution)/shard_map/all_to_all | solution.py:57

commit v2 on v1

v2 whole, which is shorter than its diff:
```python
import jax
import jax.numpy as jnp
from jax import lax
from jax.experimental import pallas as pl
from jax.experimental.pallas import tpu as pltpu
from jax.sharding import Mesh, PartitionSpec as P

TILE = 512
AXES = ("x", "zl", "y", "zh", "c")
SIZES = (4, 4, 4, 4, 2)
SMEM = pl.BlockSpec(memory_space=pltpu.SMEM)
VMEM = pl.BlockSpec(memory_space=pltpu.VMEM)
SWAP = [(0, 1), (1, 0)]
CORE = 0
OWN = 1
OTHER = 20


def tile_kernel(table_ref, panel_ref, own_ref, other_ref, partial_ref, acc_ref):
    acc_ref[...] = jnp.zeros_like(acc_ref)
    core = table_ref[CORE]
    slots = own_ref.shape[0]
    for tiles_ref, start, parity in ((own_ref, OWN, core), (other_ref, OTHER, 1 - core)):
        for slot in range(slots):
            row = table_ref[start + 2 * slot]
            col = table_ref[start + 2 * slot + 1]
            picked = panel_ref[col, parity]
            picked = jnp.where(slot < table_ref[start + 2 * slots], picked, jnp.zeros_like(picked))
            acc_ref[row] += lax.dot_general(
                picked, tiles_ref[slot], (((1,), (1,)), ((), ())), preferred_element_type=jnp.float32
            )
    partial_ref[...] = acc_ref[...].astype(jnp.bfloat16)


def last_kernel(
    table_ref,
    weight_ref,
    panel_ref,
    own_ref,
    other_ref,
    t0_ref,
    t1_ref,
    t2_ref,
    t3_ref,
    partial_ref,
    base_ref,
    scale_ref,
    acc_ref,
):
    base_ref[...] = (
        weight_ref[0] * t0_ref[...].astype(jnp.float32)
        + weight_ref[1] * t1_ref[...]
        + (weight_ref[2] - weight_ref[4]) * t2_ref[...]
        + weight_ref[3] * t3_ref[...]
    )
    scale_ref[...] = jnp.full(scale_ref.shape, 2.0 * weight_ref[4], jnp.float32)
    tile_kernel(table_ref, panel_ref, own_ref, other_ref, partial_ref, acc_ref)


def on_device(probes, tiles, tile_index, tile_count, coefficients):
    slabs = tiles[0, 0]
    half = probes.shape[0] // 2
    core = lax.axis_index("c").astype(jnp.int32)
    first = core == 0

    def ordered(mine, its):
        return jnp.where(first, jnp.stack([mine, its]), jnp.stack([its, mine]))

    keep = jnp.where(first, probes[:half], probes[half:])
    give = jnp.where(first, probes[half:], probes[:half])
    note = jnp.concatenate([tile_index[0, 0].reshape(-1), tile_count[0]])
    flat = jnp.pad(note.astype(jnp.bfloat16), (0, half * TILE - note.shape[0])).reshape(half, TILE)
    arrived = lax.ppermute(jnp.concatenate([give, flat]), "c", SWAP)
    field = ordered(keep, arrived[:half])
    table = jnp.concatenate([core.reshape(1), note, arrived[half, : note.shape[0]].astype(jnp.int32)])
    field, table, slabs = lax.optimization_barrier((field, table, slabs))
    others = lax.ppermute(slabs, "c", SWAP)

    rows = SIZES[2] * SIZES[3] * SIZES[4]
    partial = jax.ShapeDtypeStruct((rows, half, TILE), jnp.bfloat16)
    plane = jax.ShapeDtypeStruct((2, half, TILE), jnp.float32)
    acc = pltpu.VMEM(partial.shape, jnp.float32)
    params = pltpu.CompilerParams(vmem_limit_bytes=4 * 1024 * 1024)

    def gather(field_bf):
        copies = jnp.broadcast_to(field_bf[None], (SIZES[0] * SIZES[1],) + field_bf.shape)
        return lax.all_to_all(copies, ("x", "zl"), 0, 0, tiled=True)

    def total(parts, axis):
        arrived = lax.all_to_all(parts, axis, 0, 0, tiled=True).astype(jnp.float32)
        return (arrived[0] + arrived[1]) + (arrived[2] + arrived[3])

    def reduce(part):
        along_y = total(part.reshape(SIZES[2], -1, half, TILE), "y").astype(jnp.bfloat16)
        return total(along_y.reshape(SIZES[3], 2, half, TILE), "zh")

    following = pl.pallas_call(
        tile_kernel,
        out_shape=partial,
        in_specs=[SMEM, VMEM, VMEM, VMEM],
        out_specs=VMEM,
        scratch_shapes=[acc],
        compiler_params=params,
        name="tiles",
    )
    t1 = reduce(following(table, gather(field), slabs, others))
    t2 = 2.0 * reduce(following(table, gather(t1.astype(jnp.bfloat16)), slabs, others)) - field.astype(jnp.float32)
    t3 = 2.0 * reduce(following(table, gather(t2.astype(jnp.bfloat16)), slabs, others)) - t1

    part, base, scale = pl.pallas_call(
        last_kernel,
        out_shape=(partial, plane, plane),
        in_specs=[SMEM, SMEM] + [VMEM] * 7,
        out_specs=(VMEM, VMEM, VMEM),
        scratch_shapes=[acc],
        compiler_params=params,
        name="last",
    )(table, coefficients, gather(t3.astype(jnp.bfloat16)), slabs, others, field, t1, t2, t3)
    heat = base + scale * reduce(part)

    mine = jnp.where(first, heat[0], heat[1])
    its = lax.ppermute(jnp.where(first, heat[1], heat[0]), "c", SWAP)
    return ordered(mine, its).reshape(2 * half, TILE)


def solution(mesh):
    physical = Mesh(mesh.devices.reshape(SIZES), AXES)
    row, col = AXES[:2], AXES[2:]
    return jax.shard_map(
        on_device,
        mesh=physical,
        in_specs=(
            P(None, AXES),
            P(row, col, None, None, None),
            P(row, col, None, None),
            P(row, col),
            P(),
        ),
        out_specs=P(None, AXES),
        check_vma=False,
    )
```

time: 256 us -> 227 us (0.89); the launches traced: 252 us -> 226 us
  waiting for transfers between devices: 23.2 us -> 1.68 us
  blocking collectives: 162 us -> 183 us
  starting transfers between devices: 39.9 us -> 21.5 us
  local copies, waits for them, and re-layouts: 12.6 us -> 3.43 us
  Pallas kernels: 8.16 us -> 12.6 us
  other arithmetic: 5.47 us -> 2.55 us
    all_to_all x14 -> x12, blocking collectives: 162 us -> 183 us  [the longest x8 115 us: total(): arrived = lax.all_to_all(parts, axis, 0, 0, tiled=True).astype(jnp.float32)]
    all_to_all x2 -> x0, waiting for transfers between devices: 17.2 us -> none  [the longest x1 11.8 us: total(): arrived = lax.all_to_all(parts, axis, 0, 0, tiled=True)]
    ppermute x4 -> x3, starting transfers between devices: 32.6 us -> 21.5 us  [the longest x1 10.5 us: on_device(): its = lax.ppermute(jnp.where(first, heat[1], heat[0]), 'c', SWAP)]
    all_to_all x2 -> x0, starting transfers between devices: 7.37 us -> none  [the longest x1 4.05 us: spread(): return lax.all_to_all(copies, axis, 0, 0, tiled=True)]
    unnamed x13 -> x7, local copies, waits for them, and re-layouts: 10.1 us -> 3.12 us
    pallas_call x4, Pallas kernels: 8.16 us -> 12.6 us  [the longest x1 3.17 us: on_device(): pl.pallas_call(last_kernel, out_shape=(partial, plane, plane), in_specs=[...]
    ppermute x4 -> x3, waiting for transfers between devices: 6.06 us -> 1.68 us  [the longest x1 0.84 us: on_device(): its = lax.ppermute(jnp.where(first, heat[1], heat[0]), 'c', SWAP)]
    add x1, other arithmetic: 3.78 us -> 0.03 us  [on_device(): heat = base + scale * reduce(part)]
  transfers between devices with their start and end apart: 6 -> 3, of which waited for: 6 -> 2; matrix products, arithmetic and copies ran while one was open for 1% -> 0% of each run, Pallas kernels for 0% -> 0%
where the time goes in v2:
time: 227 us; the launch traced here: 226 us
  blocking collectives  183 us (81%)
  starting transfers between devices  21.5 us (9%)
  Pallas kernels  12.6 us (6%)
  local copies, waits for them, and re-layouts  3.43 us (2%)
  other arithmetic  2.55 us (1%)
    all_to_all x8, blocking collectives, total(): arrived = lax.all_to_all(parts, axis, 0, 0, tiled=True).astype(jnp.float32)  115 us
    all_to_all x4, blocking collectives, gather(): return lax.all_to_all(copies, ('x', 'zl'), 0, 0, tiled=True)  68.5 us
    ppermute x1, starting transfers between devices, on_device(): its = lax.ppermute(jnp.where(first, heat[1], heat[0]), 'c', SWAP)  10.5 us
    ppermute x1, starting transfers between devices, on_device(): arrived = lax.ppermute(jnp.concatenate([give, flat]), 'c', SWAP)  8.79 us
  transfers between devices with their start and end apart: 3, of which 2 were waited for; matrix products, arithmetic and copies ran while one was open for 0% of the time, Pallas kernels for 0%

profile of v2, /device:TPU:1, one launch (start us, length us, event | category | flops | bytes accessed | tf_op | source)
XLA Modules:
  0.0 226.2 jit_solution(1439497589646881881)
XLA Ops:
  0.7 0.8 copy.7
  1.6 0.7 select_bitcast_fusion.1
  2.4 8.8 %collective-permute-start = (bf16[32,512]{1,0:T(8,128)(2,1)S(1)}, bf16[32,512]{1,0:T(8,128)(2,1)S(1)}, u32[]{:S(2)}, u32[]{:S(2)}) collective-permute-start(bf16[32,512]{1,0:T(8,128)(2,1)S(1)} %pad_maximum_fusion), channel_id=1, source_target_pairs={{0,1},{1,0},{2,3},{3,2},{4,5},{5,4},{6,7},{7,6},{8,9},{9,8},{10,11... | collective-permute-start | bytes 98312 | tf_op jit(solution)/shard_map/ppermute | solution.py:73
  11.2 0.8 collective-permute-done
  12.1 2.2 collective-permute-start.1
  14.4 18.5 %all_to_all.60.panel_ref = bf16[16,2,16,512]{3,2,1,0:T(8,128)(2,1)S(1)} all-to-all(bf16[16,2,16,512]{3,2,1,0:T(8,128)(2,1)S(1)} %broadcast_in_dim.12), channel_id=1, replica_groups=mesh['x'=4,'zl'=4,'y'=4,'zh'=4,'c'=2] {'x','zl'}, dimensions={0} | all-to-all | bytes 1048576 | tf_op jit(solution)/shard_map/all_to_all | solution.py:87
  32.9 2.3 %copy-done = bf16[1,1,9,512,512]{4,3,2,1,0:T(8,128)(2,1)S(1)} copy-done((bf16[1,1,9,512,512]{4,3,2,1,0:T(8,128)(2,1)S(1)}, bf16[1,1,9,512,512]{4,3,2,1,0:T(8,128)(2,1)}, u32[]{:S(2)}) %copy-start) | copy-done | bytes 4718616
  35.3 3.2 %tiles.3 = bf16[32,16,512]{2,1,0:T(8,128)(2,1)S(1)} custom-call(s32[39]{0:T(128)S(1)} %pad_add_fusion.table_ref, bf16[16,2,16,512]{3,2,1,0:T(8,128)(2,1)S(1)} %all_to_all.60.panel_ref, bf16[9,512,512]{2,1,0:T(8,128)(2,1)S(1)} %bitcast.46, bf16[9,512,512]{2,1,0:T(8,128)(2,1)S(1)} %collective-permute-done.1.other_ref), custom_call_target="tpu_custom_call" | custom-call | tf_op jit(solution)/shard_map/tiles/pallas_call | solution.py:106
  38.5 11.9 %all_to_all.61 = bf16[4,8,16,512]{3,2,1,0:T(8,128)(2,1)S(1)} all-to-all(bf16[4,8,16,512]{3,2,1,0:T(8,128)(2,1)S(1)} %bitcast.50), channel_id=1, replica_groups=mesh['x'=4,'zl'=4,'y'=4,'zh'=4,'c'=2] {'y'}, dimensions={0} | all-to-all | bytes 1048576 | tf_op jit(solution)/shard_map/all_to_all | solution.py:90
  50.6 24.5 %all_to_all.62 = bf16[4,2,16,512]{3,2,1,0:T(8,128)(2,1)S(1)} all-to-all(bf16[4,2,16,512]{3,2,1,0:T(8,128)(2,1)S(1)} %bitcast.55), channel_id=1, replica_groups=mesh['x'=4,'zl'=4,'y'=4,'zh'=4,'c'=2] {'zh'}, dimensions={0} | all-to-all | bytes 262144 | tf_op jit(solution)/shard_map/all_to_all | solution.py:90
  75.2 17.8 %all_to_all.63.panel_ref = bf16[16,2,16,512]{3,2,1,0:T(8,128)(2,1)S(1)} all-to-all(bf16[16,2,16,512]{3,2,1,0:T(8,128)(2,1)S(1)} %broadcast_in_dim.14), channel_id=1, replica_groups=mesh['x'=4,'zl'=4,'y'=4,'zh'=4,'c'=2] {'x','zl'}, dimensions={0} | all-to-all | bytes 1048576 | tf_op jit(solution)/shard_map/all_to_all | solution.py:87
  93.0 3.2 %tiles.4 = bf16[32,16,512]{2,1,0:T(8,128)(2,1)S(1)} custom-call(s32[39]{0:T(128)S(1)} %pad_add_fusion.table_ref, bf16[16,2,16,512]{3,2,1,0:T(8,128)(2,1)S(1)} %all_to_all.63.panel_ref, bf16[9,512,512]{2,1,0:T(8,128)(2,1)S(1)} %bitcast.47, bf16[9,512,512]{2,1,0:T(8,128)(2,1)S(1)} %collective-permute-done.1.other_ref), custom_call_target="tpu_custom_call" | custom-call | tf_op jit(solution)/shard_map/tiles/pallas_call | solution.py:107
  96.2 9.3 %all_to_all.64 = bf16[4,8,16,512]{3,2,1,0:T(8,128)(2,1)S(1)} all-to-all(bf16[4,8,16,512]{3,2,1,0:T(8,128)(2,1)S(1)} %bitcast.51), channel_id=1, replica_groups=mesh['x'=4,'zl'=4,'y'=4,'zh'=4,'c'=2] {'y'}, dimensions={0} | all-to-all | bytes 1048576 | tf_op jit(solution)/shard_map/all_to_all | solution.py:90
  105.7 17.3 %all_to_all.65 = bf16[4,2,16,512]{3,2,1,0:T(8,128)(2,1)S(1)} all-to-all(bf16[4,2,16,512]{3,2,1,0:T(8,128)(2,1)S(1)} %bitcast.56), channel_id=1, replica_groups=mesh['x'=4,'zl'=4,'y'=4,'zh'=4,'c'=2] {'zh'}, dimensions={0} | all-to-all | bytes 262144 | tf_op jit(solution)/shard_map/all_to_all | solution.py:90
  123.1 16.0 %all_to_all.66.panel_ref = bf16[16,2,16,512]{3,2,1,0:T(8,128)(2,1)S(1)} all-to-all(bf16[16,2,16,512]{3,2,1,0:T(8,128)(2,1)S(1)} %broadcast_in_dim.15), channel_id=1, replica_groups=mesh['x'=4,'zl'=4,'y'=4,'zh'=4,'c'=2] {'x','zl'}, dimensions={0} | all-to-all | bytes 1048576 | tf_op jit(solution)/shard_map/all_to_all | solution.py:87
  139.1 3.2 %tiles.5 = bf16[32,16,512]{2,1,0:T(8,128)(2,1)S(1)} custom-call(s32[39]{0:T(128)S(1)} %pad_add_fusion.table_ref, bf16[16,2,16,512]{3,2,1,0:T(8,128)(2,1)S(1)} %all_to_all.66.panel_ref, bf16[9,512,512]{2,1,0:T(8,128)(2,1)S(1)} %bitcast.48, bf16[9,512,512]{2,1,0:T(8,128)(2,1)S(1)} %collective-permute-done.1.other_ref), custom_call_target="tpu_custom_call" | custom-call | tf_op jit(solution)/shard_map/tiles/pallas_call | solution.py:108
  142.3 9.3 %all_to_all.67 = bf16[4,8,16,512]{3,2,1,0:T(8,128)(2,1)S(1)} all-to-all(bf16[4,8,16,512]{3,2,1,0:T(8,128)(2,1)S(1)} %bitcast.52), channel_id=1, replica_groups=mesh['x'=4,'zl'=4,'y'=4,'zh'=4,'c'=2] {'y'}, dimensions={0} | all-to-all | bytes 1048576 | tf_op jit(solution)/shard_map/all_to_all | solution.py:90
  151.9 18.3 %all_to_all.68 = bf16[4,2,16,512]{3,2,1,0:T(8,128)(2,1)S(1)} all-to-all(bf16[4,2,16,512]{3,2,1,0:T(8,128)(2,1)S(1)} %bitcast.57), channel_id=1, replica_groups=mesh['x'=4,'zl'=4,'y'=4,'zh'=4,'c'=2] {'zh'}, dimensions={0} | all-to-all | bytes 262144 | tf_op jit(solution)/shard_map/all_to_all | solution.py:90
  170.3 16.1 %all_to_all.69.panel_ref = bf16[16,2,16,512]{3,2,1,0:T(8,128)(2,1)S(1)} all-to-all(bf16[16,2,16,512]{3,2,1,0:T(8,128)(2,1)S(1)} %broadcast_in_dim.33), channel_id=1, replica_groups=mesh['x'=4,'zl'=4,'y'=4,'zh'=4,'c'=2] {'x','zl'}, dimensions={0} | all-to-all | bytes 1048576 | tf_op jit(solution)/shard_map/all_to_all | solution.py:87
  186.4 3.2 %last.1 = (bf16[32,16,512]{2,1,0:T(8,128)(2,1)S(1)}, f32[2,16,512]{2,1,0:T(8,128)S(1)}, f32[2,16,512]{2,1,0:T(8,128)S(1)}) custom-call(s32[39]{0:T(128)S(1)} %pad_add_fusion.table_ref, f32[5]{0:T(128)S(1)} %copy-done.2, bf16[16,2,16,512]{3,2,1,0:T(8,128)(2,1)S(1)} %all_to_all.69.panel_ref, bf16[9,512,512]{2,1,0:T(8,128)(2,1)S(1)} %bitcast.49, ...), custom_call_target="tpu_custom_call" | custom-call | tf_op jit(solution)/shard_map/last/pallas_call | solution.py:110
  189.6 9.3 %all_to_all.70 = bf16[4,8,16,512]{3,2,1,0:T(8,128)(2,1)S(1)} all-to-all(bf16[4,8,16,512]{3,2,1,0:T(8,128)(2,1)S(1)} %bitcast.54), channel_id=1, replica_groups=mesh['x'=4,'zl'=4,'y'=4,'zh'=4,'c'=2] {'y'}, dimensions={0} | all-to-all | bytes 1048576 | tf_op jit(solution)/shard_map/all_to_all | solution.py:90
  199.2 15.0 %all_to_all.71 = bf16[4,2,16,512]{3,2,1,0:T(8,128)(2,1)S(1)} all-to-all(bf16[4,2,16,512]{3,2,1,0:T(8,128)(2,1)S(1)} %bitcast.58), channel_id=1, replica_groups=mesh['x'=4,'zl'=4,'y'=4,'zh'=4,'c'=2] {'zh'}, dimensions={0} | all-to-all | bytes 262144 | tf_op jit(solution)/shard_map/all_to_all | solution.py:90
  214.3 10.5 %collective-permute-start.2 = (f32[16,512]{1,0:T(8,128)S(1)}, f32[16,512]{1,0:T(8,128)S(1)}, u32[]{:S(2)}, u32[]{:S(2)}) collective-permute-start(f32[16,512]{1,0:T(8,128)S(1)} %get-tuple-element.24), channel_id=1, source_target_pairs={{0,1},{1,0},{2,3},{3,2},{4,5},{5,4},{6,7},{7,6},{8,9},{9,8},{10,11... | collective-permute-start | bytes 98312 | tf_op jit(solution)/shard_map/ppermute | solution.py:122
  224.7 0.8 collective-permute-done.2
  (38 shorter events, 2.1 us)
Async XLA Ops:
  2.4 9.6 %collective-permute-start = (bf16[32,512]{1,0:T(8,128)(2,1)S(1)}, bf16[32,512]{1,0:T(8,128)(2,1)S(1)}, u32[]{:S(2)}, u32[]{:S(2)}) collective-permute-start(bf16[32,512]{1,0:T(8,128)(2,1)S(1)} %pad_maximum_fusion), channel_id=1, source_target_pairs={{0,1},{1,0},{2,3},{3,2},{4,5},{5,4},{6,7},{7,6},{8,9},{9,8},{10,11... | collective-permute-start | bytes 98312 | tf_op jit(solution)/shard_map/ppermute | solution.py:73
  12.1 20.8 %collective-permute-start.1 = (bf16[9,512,512]{2,1,0:T(8,128)(2,1)}, bf16[9,512,512]{2,1,0:T(8,128)(2,1)S(1)}, u32[]{:S(2)}, u32[]{:S(2)}) collective-permute-start(bf16[9,512,512]{2,1,0:T(8,128)(2,1)} %bitcast.45), channel_id=1, source_target_pairs={{0,1},{1,0},{2,3},{3,2},{4,5},{5,4},{6,7},{7,6},{8,9},{9,8},{10,11... | collective-permute-start | bytes 14155784 | tf_op jit(solution)/shard_map/ppermute | solution.py:77
  32.9 2.3 %copy-start = (bf16[1,1,9,512,512]{4,3,2,1,0:T(8,128)(2,1)S(1)}, bf16[1,1,9,512,512]{4,3,2,1,0:T(8,128)(2,1)}, u32[]{:S(2)}) copy-start(bf16[1,1,9,512,512]{4,3,2,1,0:T(8,128)(2,1)} %param.6) | copy-start | bytes 14155780
  38.4 54.6 %copy-start.1 = (bf16[1,1,9,512,512]{4,3,2,1,0:T(8,128)(2,1)S(1)}, bf16[1,1,9,512,512]{4,3,2,1,0:T(8,128)(2,1)}, u32[]{:S(2)}) copy-start(bf16[1,1,9,512,512]{4,3,2,1,0:T(8,128)(2,1)} %param.6) | copy-start | bytes 14155780
  142.3 44.1 %copy-start.2 = (f32[5]{0:T(128)S(1)}, f32[5]{0:T(128)}, u32[]{:S(2)}) copy-start(f32[5]{0:T(128)} %weight_ref.1) | copy-start | bytes 64
  214.3 11.3 %collective-permute-start.2 = (f32[16,512]{1,0:T(8,128)S(1)}, f32[16,512]{1,0:T(8,128)S(1)}, u32[]{:S(2)}, u32[]{:S(2)}) collective-permute-start(f32[16,512]{1,0:T(8,128)S(1)} %get-tuple-element.24), channel_id=1, source_target_pairs={{0,1},{1,0},{2,3},{3,2},{4,5},{5,4},{6,7},{7,6},{8,9},{9,8},{10,11... | collective-permute-start | bytes 98312 | tf_op jit(solution)/shard_map/ppermute | solution.py:122

commit v3 on v2

--- a/solution.py
+++ b/solution.py
@@ -11,25 +11,42 @@
 SMEM = pl.BlockSpec(memory_space=pltpu.SMEM)
 VMEM = pl.BlockSpec(memory_space=pltpu.VMEM)
 SWAP = [(0, 1), (1, 0)]
-CORE = 0
-OWN = 1
-OTHER = 20
+ROW, COL, COUNT, CORE, NOTE = 0, 1, 2, 3, 4
+
+
+def add_tiles(table_ref, panel_ref, groups, partial_ref, acc_ref):
+    acc_ref[...] = jnp.zeros_like(acc_ref)
+    for note, slots, tile_of in groups:
+        parity = table_ref[note + CORE, 0]
+        for slot in range(slots):
+            row = table_ref[note + ROW, slot]
+            col = table_ref[note + COL, slot]
+            picked = panel_ref[col % SIZES[1], col // SIZES[1], parity]
+            picked = jnp.where(slot < table_ref[note + COUNT, 0], picked, jnp.zeros_like(picked))
+            acc_ref[row] += lax.dot_general(
+                picked, tile_of(slot), (((1,), (1,)), ((), ())), preferred_element_type=jnp.float32
+            )
+    partial_ref[...] = acc_ref[...].astype(jnp.bfloat16)
+
+
+def first_kernel(table_ref, panel_ref, own_ref, other_ref, partial_ref, acc_ref, held_ref, sems):
+    slots = own_ref.shape[0]
+    copies = [pltpu.make_async_copy(own_ref.at[slot], held_ref.at[slot], sems.at[slot]) for slot in range(slots)]
+    for copy in copies:
+        copy.start()
+
+    def held(slot):
+        copies[slot].wait()
+        return held_ref[slot]
+
+    groups = (NOTE, slots, lambda slot: other_ref[slot]), (0, slots, held)
+    add_tiles(table_ref, panel_ref, groups, partial_ref, acc_ref)
 
 
 def tile_kernel(table_ref, panel_ref, own_ref, other_ref, partial_ref, acc_ref):
-    acc_ref[...] = jnp.zeros_like(acc_ref)
-    core = table_ref[CORE]
     slots = own_ref.shape[0]
-    for tiles_ref, start, parity in ((own_ref, OWN, core), (other_ref, OTHER, 1 - core)):
-        for slot in range(slots):
-            row = table_ref[start + 2 * slot]
-            col = table_ref[start + 2 * slot + 1]
-            picked = panel_ref[col, parity]
-            picked = jnp.where(slot < table_ref[start + 2 * slots], picked, jnp.zeros_like(picked))
-            acc_ref[row] += lax.dot_general(
-                picked, tiles_ref[slot], (((1,), (1,)), ((), ())), preferred_element_type=jnp.float32
-            )
-    partial_ref[...] = acc_ref[...].astype(jnp.bfloat16)
+    groups = (NOTE, slots, lambda slot: other_ref[slot]), (0, slots, lambda slot: own_ref[slot])
+    add_tiles(table_ref, panel_ref, groups, partial_ref, acc_ref)
 
 
 def last_kernel(
@@ -68,11 +85,18 @@
 
     keep = jnp.where(first, probes[:half], probes[half:])
     give = jnp.where(first, probes[half:], probes[:half])
-    note = jnp.concatenate([tile_index[0, 0].reshape(-1), tile_count[0]])
-    flat = jnp.pad(note.astype(jnp.bfloat16), (0, half * TILE - note.shape[0])).reshape(half, TILE)
-    arrived = lax.ppermute(jnp.concatenate([give, flat]), "c", SWAP)
+    slots = slabs.shape[0]
+    note = jnp.concatenate(
+        [
+            tile_index[0, 0].T,
+            jnp.broadcast_to(tile_count, (1, slots)),
+            jnp.broadcast_to(core, (1, slots)),
+        ]
+    ).astype(jnp.bfloat16)
+    send = jnp.concatenate([give, jnp.pad(note, ((0, half - NOTE), (0, TILE - slots)))])
+    arrived = lax.ppermute(send, "c", SWAP)
     field = ordered(keep, arrived[:half])
-    table = jnp.concatenate([core.reshape(1), note, arrived[half, : note.shape[0]].astype(jnp.int32)])
+    table = jnp.concatenate([note, arrived[half : half + NOTE, :slots]]).astype(jnp.int32)
     field, table, slabs = lax.optimization_barrier((field, table, slabs))
     others = lax.ppermute(slabs, "c", SWAP)
 
@@ -83,17 +107,30 @@
     params = pltpu.CompilerParams(vmem_limit_bytes=4 * 1024 * 1024)
 
     def gather(field_bf):
-        copies = jnp.broadcast_to(field_bf[None], (SIZES[0] * SIZES[1],) + field_bf.shape)
-        return lax.all_to_all(copies, ("x", "zl"), 0, 0, tiled=True)
+        copies = jnp.broadcast_to(field_bf[None], (SIZES[1] * SIZES[0],) + field_bf.shape)
+        panel = lax.all_to_all(copies, ("zl", "x"), 0, 0, tiled=True)
+        return panel.reshape((SIZES[1], SIZES[0]) + field_bf.shape)
 
     def total(parts, axis):
-        arrived = lax.all_to_all(parts, axis, 0, 0, tiled=True).astype(jnp.float32)
-        return (arrived[0] + arrived[1]) + (arrived[2] + arrived[3])
+        arrived = lax.all_to_all(parts, axis, 0, 0, tiled=True)
+        a, b, c, d = (arrived[k].astype(jnp.float32) for k in range(4))
+        return (a + b) + (c + d)
 
     def reduce(part):
         along_y = total(part.reshape(SIZES[2], -1, half, TILE), "y").astype(jnp.bfloat16)
         return total(along_y.reshape(SIZES[3], 2, half, TILE), "zh")
 
+    t1 = reduce(
+        pl.pallas_call(
+            first_kernel,
+            out_shape=partial,
+            in_specs=[SMEM, VMEM, pl.BlockSpec(memory_space=pltpu.HBM), VMEM],
+            out_specs=VMEM,
+            scratch_shapes=[acc, pltpu.VMEM(slabs.shape, slabs.dtype), pltpu.SemaphoreType.DMA((slots,))],
+            compiler_params=pltpu.CompilerParams(vmem_limit_bytes=16 * 1024 * 1024),
+            name="first",
+        )(table, gather(field), pltpu.with_memory_space_constraint(slabs, pltpu.HBM), others)
+    )
     following = pl.pallas_call(
         tile_kernel,
         out_shape=partial,
@@ -103,9 +140,15 @@
         compiler_params=params,
         name="tiles",
     )
-    t1 = reduce(following(table, gather(field), slabs, others))
-    t2 = 2.0 * reduce(following(table, gather(t1.astype(jnp.bfloat16)), slabs, others)) - field.astype(jnp.float32)
-    t3 = 2.0 * reduce(following(table, gather(t2.astype(jnp.bfloat16)), slabs, others)) - t1
+
+    def settled(value):
+        return lax.optimization_barrier((value, value.astype(jnp.bfloat16)))
+
+    t1, field_1 = settled(t1)
+    t2 = 2.0 * reduce(following(table, gather(field_1), slabs, others)) - field.astype(jnp.float32)
+    t2, field_2 = settled(t2)
+    t3 = 2.0 * reduce(following(table, gather(field_2), slabs, others)) - t1
+    t3, field_3 = settled(t3)
 
     part, base, scale = pl.pallas_call(
         last_kernel,
@@ -115,7 +158,7 @@
         scratch_shapes=[acc],
         compiler_params=params,
         name="last",
-    )(table, coefficients, gather(t3.astype(jnp.bfloat16)), slabs, others, field, t1, t2, t3)
+    )(table, coefficients, gather(field_3), slabs, others, field, t1, t2, t3)
     heat = base + scale * reduce(part)
 
     mine = jnp.where(first, heat[0], heat[1])

time: 227 us -> 221 us (0.974)
  blocking collectives: 183 us -> 174 us
  starting transfers between devices: 21.5 us -> 26.3 us
  local copies, waits for them, and re-layouts: 3.43 us -> 0.22 us
  Pallas kernels: 12.6 us -> 14.9 us
    all_to_all x12, blocking collectives: 183 us -> 174 us  [the longest x8 108 us: total(): arrived = lax.all_to_all(parts, axis, 0, 0, tiled=True)]
    ppermute x1, starting transfers between devices: 10.5 us -> 15.2 us  [on_device(): its = lax.ppermute(jnp.where(first, heat[1], heat[0]), 'c', SWAP)]
    unnamed x7 -> x6, local copies, waits for them, and re-layouts: 3.12 us -> 0.01 us
where the time goes in v3:
time: 221 us; the launch traced here: 220 us
  blocking collectives  174 us (79%)
  starting transfers between devices  26.3 us (12%)
  Pallas kernels  14.9 us (7%)
  other arithmetic  2.51 us (1%)
    all_to_all x8, blocking collectives, total(): arrived = lax.all_to_all(parts, axis, 0, 0, tiled=True)  108 us
    all_to_all x4, blocking collectives, gather(): panel = lax.all_to_all(copies, ('zl', 'x'), 0, 0, tiled=True)  66 us
    ppermute x1, starting transfers between devices, on_device(): its = lax.ppermute(jnp.where(first, heat[1], heat[0]), 'c', SWAP)  15.2 us
    ppermute x1, starting transfers between devices, on_device(): arrived = lax.ppermute(send, 'c', SWAP)  8.79 us
    pallas_call x1, Pallas kernels, on_device(): pl.pallas_call(first_kernel, out_shape=partial, in_specs=[SMEM, VMEM, pl....  5.25 us
  transfers between devices with their start and end apart: 3, of which 2 were waited for; matrix products, arithmetic and copies ran while one was open for 0% of the time, Pallas kernels for 0%

profile of v3, /device:TPU:1, one launch (start us, length us, event | category | flops | bytes accessed | tf_op | source)
XLA Modules:
  0.0 220.3 jit_solution(7499318348588624989)
XLA Ops:
  0.7 0.7 convert_bitcast_fusion
  1.3 0.7 select_bitcast_fusion.1
  2.1 8.8 %collective-permute-start = (bf16[32,512]{1,0:T(8,128)(2,1)S(1)}, bf16[32,512]{1,0:T(8,128)(2,1)S(1)}, u32[]{:S(2)}, u32[]{:S(2)}) collective-permute-start(bf16[32,512]{1,0:T(8,128)(2,1)S(1)} %pad_maximum_fusion), channel_id=1, source_target_pairs={{0,1},{1,0},{2,3},{3,2},{4,5},{5,4},{6,7},{7,6},{8,9},{9,8},{10,11... | collective-permute-start | bytes 98312 | tf_op jit(solution)/shard_map/ppermute | solution.py:97
  10.9 0.8 collective-permute-done
  11.8 2.3 %collective-permute-start.1 = (bf16[9,512,512]{2,1,0:T(8,128)(2,1)}, bf16[9,512,512]{2,1,0:T(8,128)(2,1)S(1)}, u32[]{:S(2)}, u32[]{:S(2)}) collective-permute-start(bf16[9,512,512]{2,1,0:T(8,128)(2,1)} %bitcast.39), channel_id=1, source_target_pairs={{0,1},{1,0},{2,3},{3,2},{4,5},{5,4},{6,7},{7,6},{8,9},{9,8},{10,11... | collective-permute-start | bytes 14155784 | tf_op jit(solution)/shard_map/ppermute | solution.py:101
  14.1 16.9 %all_to_all.60 = bf16[16,2,16,512]{3,2,1,0:T(8,128)(2,1)S(1)} all-to-all(bf16[16,2,16,512]{3,2,1,0:T(8,128)(2,1)S(1)} %broadcast_in_dim.17), channel_id=1, replica_groups=mesh['x'=4,'zl'=4,'y'=4,'zh'=4,'c'=2] {'zl','x'}, dimensions={0} | all-to-all | bytes 1048576 | tf_op jit(solution)/shard_map/all_to_all | solution.py:111
  31.1 5.2 %first.1 = bf16[32,16,512]{2,1,0:T(8,128)(2,1)S(1)} custom-call(s32[8,9]{1,0:T(8,128)S(1)} %maximum_convert_fusion.table_ref, bf16[4,4,2,16,512]{4,3,2,1,0:T(8,128)(2,1)S(1)} %bitcast.47, bf16[9,512,512]{2,1,0:T(8,128)(2,1)} %bitcast.40, bf16[9,512,512]{2,1,0:T(8,128)(2,1)S(1)} %collective-permute-done.1.other_ref), custom_call_target="tpu_custom_call" | custom-call | tf_op jit(solution)/shard_map/first/pallas_call | solution.py:124
  36.3 11.0 %all_to_all.61 = bf16[4,8,16,512]{3,2,1,0:T(8,128)(2,1)S(1)} all-to-all(bf16[4,8,16,512]{3,2,1,0:T(8,128)(2,1)S(1)} %bitcast.48), channel_id=1, replica_groups=mesh['x'=4,'zl'=4,'y'=4,'zh'=4,'c'=2] {'y'}, dimensions={0} | all-to-all | bytes 1048576 | tf_op jit(solution)/shard_map/all_to_all | solution.py:115
  47.4 24.2 %all_to_all.62 = bf16[4,2,16,512]{3,2,1,0:T(8,128)(2,1)S(1)} all-to-all(bf16[4,2,16,512]{3,2,1,0:T(8,128)(2,1)S(1)} %bitcast.54), channel_id=1, replica_groups=mesh['x'=4,'zl'=4,'y'=4,'zh'=4,'c'=2] {'zh'}, dimensions={0} | all-to-all | bytes 262144 | tf_op jit(solution)/shard_map/all_to_all | solution.py:115
  71.6 17.0 %all_to_all.63 = bf16[16,2,16,512]{3,2,1,0:T(8,128)(2,1)S(1)} all-to-all(bf16[16,2,16,512]{3,2,1,0:T(8,128)(2,1)S(1)} %broadcast_in_dim.18), channel_id=1, replica_groups=mesh['x'=4,'zl'=4,'y'=4,'zh'=4,'c'=2] {'zl','x'}, dimensions={0} | all-to-all | bytes 1048576 | tf_op jit(solution)/shard_map/all_to_all | solution.py:111
  88.7 3.2 %tiles.2 = bf16[32,16,512]{2,1,0:T(8,128)(2,1)S(1)} custom-call(s32[8,9]{1,0:T(8,128)S(1)} %maximum_convert_fusion.table_ref, bf16[4,4,2,16,512]{4,3,2,1,0:T(8,128)(2,1)S(1)} %bitcast.49, bf16[9,512,512]{2,1,0:T(8,128)(2,1)S(1)} %bitcast.43, bf16[9,512,512]{2,1,0:T(8,128)(2,1)S(1)} %collective-permute-done.1.other_ref), custom_call_target="tpu_custom_call" | custom-call | tf_op jit(solution)/shard_map/tiles/pallas_call | solution.py:148
  91.9 9.3 %all_to_all.64 = bf16[4,8,16,512]{3,2,1,0:T(8,128)(2,1)S(1)} all-to-all(bf16[4,8,16,512]{3,2,1,0:T(8,128)(2,1)S(1)} %bitcast.50), channel_id=1, replica_groups=mesh['x'=4,'zl'=4,'y'=4,'zh'=4,'c'=2] {'y'}, dimensions={0} | all-to-all | bytes 1048576 | tf_op jit(solution)/shard_map/all_to_all | solution.py:115
  101.3 15.8 %all_to_all.65 = bf16[4,2,16,512]{3,2,1,0:T(8,128)(2,1)S(1)} all-to-all(bf16[4,2,16,512]{3,2,1,0:T(8,128)(2,1)S(1)} %bitcast.55), channel_id=1, replica_groups=mesh['x'=4,'zl'=4,'y'=4,'zh'=4,'c'=2] {'zh'}, dimensions={0} | all-to-all | bytes 262144 | tf_op jit(solution)/shard_map/all_to_all | solution.py:115
  117.2 17.4 %all_to_all.66 = bf16[16,2,16,512]{3,2,1,0:T(8,128)(2,1)S(1)} all-to-all(bf16[16,2,16,512]{3,2,1,0:T(8,128)(2,1)S(1)} %broadcast_in_dim.19), channel_id=1, replica_groups=mesh['x'=4,'zl'=4,'y'=4,'zh'=4,'c'=2] {'zl','x'}, dimensions={0} | all-to-all | bytes 1048576 | tf_op jit(solution)/shard_map/all_to_all | solution.py:111
  134.6 3.2 %tiles.3 = bf16[32,16,512]{2,1,0:T(8,128)(2,1)S(1)} custom-call(s32[8,9]{1,0:T(8,128)S(1)} %maximum_convert_fusion.table_ref, bf16[4,4,2,16,512]{4,3,2,1,0:T(8,128)(2,1)S(1)} %bitcast.51, bf16[9,512,512]{2,1,0:T(8,128)(2,1)S(1)} %bitcast.44, bf16[9,512,512]{2,1,0:T(8,128)(2,1)S(1)} %collective-permute-done.1.other_ref), custom_call_target="tpu_custom_call" | custom-call | tf_op jit(solution)/shard_map/tiles/pallas_call | solution.py:150
  137.9 9.3 %all_to_all.67 = bf16[4,8,16,512]{3,2,1,0:T(8,128)(2,1)S(1)} all-to-all(bf16[4,8,16,512]{3,2,1,0:T(8,128)(2,1)S(1)} %bitcast.52), channel_id=1, replica_groups=mesh['x'=4,'zl'=4,'y'=4,'zh'=4,'c'=2] {'y'}, dimensions={0} | all-to-all | bytes 1048576 | tf_op jit(solution)/shard_map/all_to_all | solution.py:115
  147.3 14.4 %all_to_all.68 = bf16[4,2,16,512]{3,2,1,0:T(8,128)(2,1)S(1)} all-to-all(bf16[4,2,16,512]{3,2,1,0:T(8,128)(2,1)S(1)} %bitcast.56), channel_id=1, replica_groups=mesh['x'=4,'zl'=4,'y'=4,'zh'=4,'c'=2] {'zh'}, dimensions={0} | all-to-all | bytes 262144 | tf_op jit(solution)/shard_map/all_to_all | solution.py:115
  161.8 14.5 %all_to_all.69 = bf16[16,2,16,512]{3,2,1,0:T(8,128)(2,1)S(1)} all-to-all(bf16[16,2,16,512]{3,2,1,0:T(8,128)(2,1)S(1)} %broadcast_in_dim.40), channel_id=1, replica_groups=mesh['x'=4,'zl'=4,'y'=4,'zh'=4,'c'=2] {'zl','x'}, dimensions={0} | all-to-all | bytes 1048576 | tf_op jit(solution)/shard_map/all_to_all | solution.py:111
  176.3 3.2 %last.1 = (bf16[32,16,512]{2,1,0:T(8,128)(2,1)S(1)}, f32[2,16,512]{2,1,0:T(8,128)S(1)}, f32[2,16,512]{2,1,0:T(8,128)S(1)}) custom-call(s32[8,9]{1,0:T(8,128)S(1)} %maximum_convert_fusion.table_ref, f32[5]{0:T(128)S(1)} %copy-done, bf16[4,4,2,16,512]{4,3,2,1,0:T(8,128)(2,1)S(1)} %bitcast.46, bf16[9,512,512]{2,1,0:T(8,128)(2,1)S(1)} %bitcast.45, ...), custom_call_target="tpu_custom_call" | custom-call | tf_op jit(solution)/shard_map/last/pallas_call | solution.py:153
  179.6 9.3 %all_to_all.70 = bf16[4,8,16,512]{3,2,1,0:T(8,128)(2,1)S(1)} all-to-all(bf16[4,8,16,512]{3,2,1,0:T(8,128)(2,1)S(1)} %bitcast.53), channel_id=1, replica_groups=mesh['x'=4,'zl'=4,'y'=4,'zh'=4,'c'=2] {'y'}, dimensions={0} | all-to-all | bytes 1048576 | tf_op jit(solution)/shard_map/all_to_all | solution.py:115
  189.0 14.6 %all_to_all.71 = bf16[4,2,16,512]{3,2,1,0:T(8,128)(2,1)S(1)} all-to-all(bf16[4,2,16,512]{3,2,1,0:T(8,128)(2,1)S(1)} %bitcast.57), channel_id=1, replica_groups=mesh['x'=4,'zl'=4,'y'=4,'zh'=4,'c'=2] {'zh'}, dimensions={0} | all-to-all | bytes 262144 | tf_op jit(solution)/shard_map/all_to_all | solution.py:115
  203.6 15.2 %collective-permute-start.2 = (f32[16,512]{1,0:T(8,128)S(1)}, f32[16,512]{1,0:T(8,128)S(1)}, u32[]{:S(2)}, u32[]{:S(2)}) collective-permute-start(f32[16,512]{1,0:T(8,128)S(1)} %get-tuple-element.36), channel_id=1, source_target_pairs={{0,1},{1,0},{2,3},{3,2},{4,5},{5,4},{6,7},{7,6},{8,9},{9,8},{10,11... | collective-permute-start | bytes 98312 | tf_op jit(solution)/shard_map/ppermute | solution.py:165
  218.8 0.8 collective-permute-done.2
  219.7 0.6 maximum_select_fusion
  (28 shorter events, 0.7 us)
Async XLA Ops:
  2.1 9.6 %collective-permute-start = (bf16[32,512]{1,0:T(8,128)(2,1)S(1)}, bf16[32,512]{1,0:T(8,128)(2,1)S(1)}, u32[]{:S(2)}, u32[]{:S(2)}) collective-permute-start(bf16[32,512]{1,0:T(8,128)(2,1)S(1)} %pad_maximum_fusion), channel_id=1, source_target_pairs={{0,1},{1,0},{2,3},{3,2},{4,5},{5,4},{6,7},{7,6},{8,9},{9,8},{10,11... | collective-permute-start | bytes 98312 | tf_op jit(solution)/shard_map/ppermute | solution.py:97
  11.8 19.3 %collective-permute-start.1 = (bf16[9,512,512]{2,1,0:T(8,128)(2,1)}, bf16[9,512,512]{2,1,0:T(8,128)(2,1)S(1)}, u32[]{:S(2)}, u32[]{:S(2)}) collective-permute-start(bf16[9,512,512]{2,1,0:T(8,128)(2,1)} %bitcast.39), channel_id=1, source_target_pairs={{0,1},{1,0},{2,3},{3,2},{4,5},{5,4},{6,7},{7,6},{8,9},{9,8},{10,11... | collective-permute-start | bytes 14155784 | tf_op jit(solution)/shard_map/ppermute | solution.py:101
  31.0 57.6 %slice-start = ((s8[4718592]{0:T(1024)(128)(4,1)}), s8[4194304]{0:T(1024)(128)(4,1)S(1)}, s32[]{:S(2)}) async-start(s8[4718592]{0:T(1024)(128)(4,1)} %bitcast.41), calls=%async_computation.12 | async-start | bytes 8388608
  31.1 57.6 %slice-start.1 = ((s8[4718592]{0:T(1024)(128)(4,1)}), s8[524288]{0:T(1024)(128)(4,1)S(1)}, s32[]{:S(2)}) async-start(s8[4718592]{0:T(1024)(128)(4,1)} %bitcast.41), calls=%async_computation.13 | async-start | bytes 1048576
  134.6 41.7 %copy-start = (f32[5]{0:T(128)S(1)}, f32[5]{0:T(128)}, u32[]{:S(2)}) copy-start(f32[5]{0:T(128)} %weight_ref.1) | copy-start | bytes 64
  203.6 16.1 %collective-permute-start.2 = (f32[16,512]{1,0:T(8,128)S(1)}, f32[16,512]{1,0:T(8,128)S(1)}, u32[]{:S(2)}, u32[]{:S(2)}) collective-permute-start(f32[16,512]{1,0:T(8,128)S(1)} %get-tuple-element.36), channel_id=1, source_target_pairs={{0,1},{1,0},{2,3},{3,2},{4,5},{5,4},{6,7},{7,6},{8,9},{9,8},{10,11... | collective-permute-start | bytes 98312 | tf_op jit(solution)/shard_map/ppermute | solution.py:165

commit v4 on v3

--- a/solution.py
+++ b/solution.py
@@ -29,7 +29,7 @@
     partial_ref[...] = acc_ref[...].astype(jnp.bfloat16)
 
 
-def first_kernel(table_ref, panel_ref, own_ref, other_ref, partial_ref, acc_ref, held_ref, sems):
+def first_kernel(table_ref, panel_ref, own_ref, other_ref, partial_ref, held_ref, acc_ref, sems):
     slots = own_ref.shape[0]
     copies = [pltpu.make_async_copy(own_ref.at[slot], held_ref.at[slot], sems.at[slot]) for slot in range(slots)]
     for copy in copies:
@@ -94,9 +94,11 @@
         ]
     ).astype(jnp.bfloat16)
     send = jnp.concatenate([give, jnp.pad(note, ((0, half - NOTE), (0, TILE - slots)))])
+    send = lax.optimization_barrier(send)
     arrived = lax.ppermute(send, "c", SWAP)
     field = ordered(keep, arrived[:half])
-    table = jnp.concatenate([note, arrived[half : half + NOTE, :slots]]).astype(jnp.int32)
+    notes = [both[half : half + NOTE, :slots] for both in (send, arrived)]
+    table = jnp.concatenate(notes).astype(jnp.int32)
     field, table, slabs = lax.optimization_barrier((field, table, slabs))
     others = lax.ppermute(slabs, "c", SWAP)
 
@@ -120,17 +122,16 @@
         along_y = total(part.reshape(SIZES[2], -1, half, TILE), "y").astype(jnp.bfloat16)
         return total(along_y.reshape(SIZES[3], 2, half, TILE), "zh")
 
-    t1 = reduce(
-        pl.pallas_call(
-            first_kernel,
-            out_shape=partial,
-            in_specs=[SMEM, VMEM, pl.BlockSpec(memory_space=pltpu.HBM), VMEM],
-            out_specs=VMEM,
-            scratch_shapes=[acc, pltpu.VMEM(slabs.shape, slabs.dtype), pltpu.SemaphoreType.DMA((slots,))],
-            compiler_params=pltpu.CompilerParams(vmem_limit_bytes=16 * 1024 * 1024),
-            name="first",
-        )(table, gather(field), pltpu.with_memory_space_constraint(slabs, pltpu.HBM), others)
-    )
+    part, held = pl.pallas_call(
+        first_kernel,
+        out_shape=(partial, jax.ShapeDtypeStruct(slabs.shape, slabs.dtype)),
+        in_specs=[SMEM, VMEM, pl.BlockSpec(memory_space=pltpu.HBM), VMEM],
+        out_specs=(VMEM, VMEM),
+        scratch_shapes=[acc, pltpu.SemaphoreType.DMA((slots,))],
+        compiler_params=params,
+        name="first",
+    )(table, gather(field), pltpu.with_memory_space_constraint(slabs, pltpu.HBM), others)
+    t1 = reduce(part)
     following = pl.pallas_call(
         tile_kernel,
         out_shape=partial,
@@ -145,9 +146,9 @@
         return lax.optimization_barrier((value, value.astype(jnp.bfloat16)))
 
     t1, field_1 = settled(t1)
-    t2 = 2.0 * reduce(following(table, gather(field_1), slabs, others)) - field.astype(jnp.float32)
+    t2 = 2.0 * reduce(following(table, gather(field_1), held, others)) - field.astype(jnp.float32)
     t2, field_2 = settled(t2)
-    t3 = 2.0 * reduce(following(table, gather(field_2), slabs, others)) - t1
+    t3 = 2.0 * reduce(following(table, gather(field_2), held, others)) - t1
     t3, field_3 = settled(t3)
 
     part, base, scale = pl.pallas_call(
@@ -158,7 +159,7 @@
         scratch_shapes=[acc],
         compiler_params=params,
         name="last",
-    )(table, coefficients, gather(field_3), slabs, others, field, t1, t2, t3)
+    )(table, coefficients, gather(field_3), held, others, field, t1, t2, t3)
     heat = base + scale * reduce(part)
 
     mine = jnp.where(first, heat[0], heat[1])

time: 221 us -> 221 us (level)
  no operation moved by 1% of the time
where the time goes in v4:
time: 221 us; the launch traced here: 220 us
  blocking collectives  174 us (79%)
  starting transfers between devices  26.2 us (12%)
  Pallas kernels  14.9 us (7%)
  other arithmetic  2.58 us (1%)
    all_to_all x8, blocking collectives, total(): arrived = lax.all_to_all(parts, axis, 0, 0, tiled=True)  108 us
    all_to_all x4, blocking collectives, gather(): panel = lax.all_to_all(copies, ('zl', 'x'), 0, 0, tiled=True)  65.9 us
    ppermute x1, starting transfers between devices, on_device(): its = lax.ppermute(jnp.where(first, heat[1], heat[0]), 'c', SWAP)  15.2 us
    ppermute x1, starting transfers between devices, on_device(): arrived = lax.ppermute(send, 'c', SWAP)  8.78 us
    pallas_call x1, Pallas kernels, on_device(): pl.pallas_call(first_kernel, out_shape=(partial, jax.ShapeDtypeStruct(sla...  5.25 us
  transfers between devices with their start and end apart: 3, of which 2 were waited for; matrix products, arithmetic and copies ran while one was open for 0% of the time, Pallas kernels for 0%

profile of v4, /device:TPU:1, one launch (start us, length us, event | category | flops | bytes accessed | tf_op | source)
XLA Modules:
  0.0 220.5 jit_solution(4067371050584691336)
XLA Ops:
  0.8 0.7 convert_bitcast_fusion
  1.5 0.7 select_bitcast_fusion.1
  2.3 8.8 %collective-permute-start = (bf16[32,512]{1,0:T(8,128)(2,1)S(1)}, bf16[32,512]{1,0:T(8,128)(2,1)S(1)}, u32[]{:S(2)}, u32[]{:S(2)}) collective-permute-start(bf16[32,512]{1,0:T(8,128)(2,1)S(1)} %fusion.2), channel_id=1, source_target_pairs={{0,1},{1,0},{2,3},{3,2},{4,5},{5,4},{6,7},{7,6},{8,9},{9,8},{10,11... | collective-permute-start | bytes 98312 | tf_op jit(solution)/shard_map/ppermute | solution.py:98
  11.1 0.8 collective-permute-done
  12.0 2.3 %collective-permute-start.1 = (bf16[9,512,512]{2,1,0:T(8,128)(2,1)}, bf16[9,512,512]{2,1,0:T(8,128)(2,1)S(1)}, u32[]{:S(2)}, u32[]{:S(2)}) collective-permute-start(bf16[9,512,512]{2,1,0:T(8,128)(2,1)} %bitcast.50), channel_id=1, source_target_pairs={{0,1},{1,0},{2,3},{3,2},{4,5},{5,4},{6,7},{7,6},{8,9},{9,8},{10,11... | collective-permute-start | bytes 14155784 | tf_op jit(solution)/shard_map/ppermute | solution.py:103
  14.3 16.9 %all_to_all.60 = bf16[16,2,16,512]{3,2,1,0:T(8,128)(2,1)S(1)} all-to-all(bf16[16,2,16,512]{3,2,1,0:T(8,128)(2,1)S(1)} %broadcast_in_dim.17), channel_id=1, replica_groups=mesh['x'=4,'zl'=4,'y'=4,'zh'=4,'c'=2] {'zl','x'}, dimensions={0} | all-to-all | bytes 1048576 | tf_op jit(solution)/shard_map/all_to_all | solution.py:113
  31.2 5.3 %first.1 = (bf16[32,16,512]{2,1,0:T(8,128)(2,1)S(1)}, bf16[9,512,512]{2,1,0:T(8,128)(2,1)S(1)}) custom-call(s32[8,9]{1,0:T(8,128)S(1)} %maximum_convert_fusion.table_ref, bf16[4,4,2,16,512]{4,3,2,1,0:T(8,128)(2,1)S(1)} %bitcast.43, bf16[9,512,512]{2,1,0:T(8,128)(2,1)} %bitcast.51, bf16[9,512,512]{2,1,0:T(8,128)(2,1)S(1)} %collective-permute-done.1.other_ref), custom_call_target="tpu_custom_call" | custom-call | tf_op jit(solution)/shard_map/first/pallas_call | solution.py:125
  36.5 11.0 %all_to_all.61 = bf16[4,8,16,512]{3,2,1,0:T(8,128)(2,1)S(1)} all-to-all(bf16[4,8,16,512]{3,2,1,0:T(8,128)(2,1)S(1)} %bitcast.49), channel_id=1, replica_groups=mesh['x'=4,'zl'=4,'y'=4,'zh'=4,'c'=2] {'y'}, dimensions={0} | all-to-all | bytes 1048576 | tf_op jit(solution)/shard_map/all_to_all | solution.py:117
  47.5 24.2 %all_to_all.62 = bf16[4,2,16,512]{3,2,1,0:T(8,128)(2,1)S(1)} all-to-all(bf16[4,2,16,512]{3,2,1,0:T(8,128)(2,1)S(1)} %bitcast.52), channel_id=1, replica_groups=mesh['x'=4,'zl'=4,'y'=4,'zh'=4,'c'=2] {'zh'}, dimensions={0} | all-to-all | bytes 262144 | tf_op jit(solution)/shard_map/all_to_all | solution.py:117
  71.8 17.0 %all_to_all.63 = bf16[16,2,16,512]{3,2,1,0:T(8,128)(2,1)S(1)} all-to-all(bf16[16,2,16,512]{3,2,1,0:T(8,128)(2,1)S(1)} %broadcast_in_dim.18), channel_id=1, replica_groups=mesh['x'=4,'zl'=4,'y'=4,'zh'=4,'c'=2] {'zl','x'}, dimensions={0} | all-to-all | bytes 1048576 | tf_op jit(solution)/shard_map/all_to_all | solution.py:113
  88.8 3.2 %tiles.2 = bf16[32,16,512]{2,1,0:T(8,128)(2,1)S(1)} custom-call(s32[8,9]{1,0:T(8,128)S(1)} %maximum_convert_fusion.table_ref, bf16[4,4,2,16,512]{4,3,2,1,0:T(8,128)(2,1)S(1)} %bitcast.44, bf16[9,512,512]{2,1,0:T(8,128)(2,1)S(1)} %get-tuple-element.24.own_ref, bf16[9,512,512]{2,1,0:T(8,128)(2,1)S(1)} %collective-permute-done.1.other_ref), custom_call_target="tpu_custom_call" | custom-call | tf_op jit(solution)/shard_map/tiles/pallas_call | solution.py:149
  92.1 9.3 %all_to_all.64 = bf16[4,8,16,512]{3,2,1,0:T(8,128)(2,1)S(1)} all-to-all(bf16[4,8,16,512]{3,2,1,0:T(8,128)(2,1)S(1)} %bitcast.45), channel_id=1, replica_groups=mesh['x'=4,'zl'=4,'y'=4,'zh'=4,'c'=2] {'y'}, dimensions={0} | all-to-all | bytes 1048576 | tf_op jit(solution)/shard_map/all_to_all | solution.py:117
  101.5 15.8 %all_to_all.65 = bf16[4,2,16,512]{3,2,1,0:T(8,128)(2,1)S(1)} all-to-all(bf16[4,2,16,512]{3,2,1,0:T(8,128)(2,1)S(1)} %bitcast.53), channel_id=1, replica_groups=mesh['x'=4,'zl'=4,'y'=4,'zh'=4,'c'=2] {'zh'}, dimensions={0} | all-to-all | bytes 262144 | tf_op jit(solution)/shard_map/all_to_all | solution.py:117
  117.4 17.4 %all_to_all.66 = bf16[16,2,16,512]{3,2,1,0:T(8,128)(2,1)S(1)} all-to-all(bf16[16,2,16,512]{3,2,1,0:T(8,128)(2,1)S(1)} %broadcast_in_dim.19), channel_id=1, replica_groups=mesh['x'=4,'zl'=4,'y'=4,'zh'=4,'c'=2] {'zl','x'}, dimensions={0} | all-to-all | bytes 1048576 | tf_op jit(solution)/shard_map/all_to_all | solution.py:113
  134.8 3.2 %tiles.3 = bf16[32,16,512]{2,1,0:T(8,128)(2,1)S(1)} custom-call(s32[8,9]{1,0:T(8,128)S(1)} %maximum_convert_fusion.table_ref, bf16[4,4,2,16,512]{4,3,2,1,0:T(8,128)(2,1)S(1)} %bitcast.46, bf16[9,512,512]{2,1,0:T(8,128)(2,1)S(1)} %get-tuple-element.24.own_ref, bf16[9,512,512]{2,1,0:T(8,128)(2,1)S(1)} %collective-permute-done.1.other_ref), custom_call_target="tpu_custom_call" | custom-call | tf_op jit(solution)/shard_map/tiles/pallas_call | solution.py:151
  138.1 9.3 %all_to_all.67 = bf16[4,8,16,512]{3,2,1,0:T(8,128)(2,1)S(1)} all-to-all(bf16[4,8,16,512]{3,2,1,0:T(8,128)(2,1)S(1)} %bitcast.47), channel_id=1, replica_groups=mesh['x'=4,'zl'=4,'y'=4,'zh'=4,'c'=2] {'y'}, dimensions={0} | all-to-all | bytes 1048576 | tf_op jit(solution)/shard_map/all_to_all | solution.py:117
  147.5 14.4 %all_to_all.68 = bf16[4,2,16,512]{3,2,1,0:T(8,128)(2,1)S(1)} all-to-all(bf16[4,2,16,512]{3,2,1,0:T(8,128)(2,1)S(1)} %bitcast.54), channel_id=1, replica_groups=mesh['x'=4,'zl'=4,'y'=4,'zh'=4,'c'=2] {'zh'}, dimensions={0} | all-to-all | bytes 262144 | tf_op jit(solution)/shard_map/all_to_all | solution.py:117
  162.0 14.5 %all_to_all.69 = bf16[16,2,16,512]{3,2,1,0:T(8,128)(2,1)S(1)} all-to-all(bf16[16,2,16,512]{3,2,1,0:T(8,128)(2,1)S(1)} %broadcast_in_dim.40), channel_id=1, replica_groups=mesh['x'=4,'zl'=4,'y'=4,'zh'=4,'c'=2] {'zl','x'}, dimensions={0} | all-to-all | bytes 1048576 | tf_op jit(solution)/shard_map/all_to_all | solution.py:113
  176.5 3.2 %last.1 = (bf16[32,16,512]{2,1,0:T(8,128)(2,1)S(1)}, f32[2,16,512]{2,1,0:T(8,128)S(1)}, f32[2,16,512]{2,1,0:T(8,128)S(1)}) custom-call(s32[8,9]{1,0:T(8,128)S(1)} %maximum_convert_fusion.table_ref, f32[5]{0:T(128)S(1)} %copy-done, bf16[4,4,2,16,512]{4,3,2,1,0:T(8,128)(2,1)S(1)} %bitcast.42, bf16[9,512,512]{2,1,0:T(8,128)(2,1)S(1)} %get-tuple-element.24.own_ref, ...), custom_call_target="tpu_custom_call" | custom-call | tf_op jit(solution)/shard_map/last/pallas_call | solution.py:154
  179.8 9.3 %all_to_all.70 = bf16[4,8,16,512]{3,2,1,0:T(8,128)(2,1)S(1)} all-to-all(bf16[4,8,16,512]{3,2,1,0:T(8,128)(2,1)S(1)} %bitcast.48), channel_id=1, replica_groups=mesh['x'=4,'zl'=4,'y'=4,'zh'=4,'c'=2] {'y'}, dimensions={0} | all-to-all | bytes 1048576 | tf_op jit(solution)/shard_map/all_to_all | solution.py:117
  189.2 14.6 %all_to_all.71 = bf16[4,2,16,512]{3,2,1,0:T(8,128)(2,1)S(1)} all-to-all(bf16[4,2,16,512]{3,2,1,0:T(8,128)(2,1)S(1)} %bitcast.55), channel_id=1, replica_groups=mesh['x'=4,'zl'=4,'y'=4,'zh'=4,'c'=2] {'zh'}, dimensions={0} | all-to-all | bytes 262144 | tf_op jit(solution)/shard_map/all_to_all | solution.py:117
  203.8 15.2 %collective-permute-start.2 = (f32[16,512]{1,0:T(8,128)S(1)}, f32[16,512]{1,0:T(8,128)S(1)}, u32[]{:S(2)}, u32[]{:S(2)}) collective-permute-start(f32[16,512]{1,0:T(8,128)S(1)} %get-tuple-element.40), channel_id=1, source_target_pairs={{0,1},{1,0},{2,3},{3,2},{4,5},{5,4},{6,7},{7,6},{8,9},{9,8},{10,11... | collective-permute-start | bytes 98312 | tf_op jit(solution)/shard_map/ppermute | solution.py:166
  219.0 0.8 collective-permute-done.2
  219.9 0.6 maximum_select_fusion
  (25 shorter events, 0.9 us)
Async XLA Ops:
  2.3 9.6 %collective-permute-start = (bf16[32,512]{1,0:T(8,128)(2,1)S(1)}, bf16[32,512]{1,0:T(8,128)(2,1)S(1)}, u32[]{:S(2)}, u32[]{:S(2)}) collective-permute-start(bf16[32,512]{1,0:T(8,128)(2,1)S(1)} %fusion.2), channel_id=1, source_target_pairs={{0,1},{1,0},{2,3},{3,2},{4,5},{5,4},{6,7},{7,6},{8,9},{9,8},{10,11... | collective-permute-start | bytes 98312 | tf_op jit(solution)/shard_map/ppermute | solution.py:98
  12.0 19.3 %collective-permute-start.1 = (bf16[9,512,512]{2,1,0:T(8,128)(2,1)}, bf16[9,512,512]{2,1,0:T(8,128)(2,1)S(1)}, u32[]{:S(2)}, u32[]{:S(2)}) collective-permute-start(bf16[9,512,512]{2,1,0:T(8,128)(2,1)} %bitcast.50), channel_id=1, source_target_pairs={{0,1},{1,0},{2,3},{3,2},{4,5},{5,4},{6,7},{7,6},{8,9},{9,8},{10,11... | collective-permute-start | bytes 14155784 | tf_op jit(solution)/shard_map/ppermute | solution.py:103
  134.8 41.7 %copy-start = (f32[5]{0:T(128)S(1)}, f32[5]{0:T(128)}, u32[]{:S(2)}) copy-start(f32[5]{0:T(128)} %weight_ref.1) | copy-start | bytes 64
  203.8 16.0 %collective-permute-start.2 = (f32[16,512]{1,0:T(8,128)S(1)}, f32[16,512]{1,0:T(8,128)S(1)}, u32[]{:S(2)}, u32[]{:S(2)}) collective-permute-start(f32[16,512]{1,0:T(8,128)S(1)} %get-tuple-element.40), channel_id=1, source_target_pairs={{0,1},{1,0},{2,3},{3,2},{4,5},{5,4},{6,7},{7,6},{8,9},{9,8},{10,11... | collective-permute-start | bytes 98312 | tf_op jit(solution)/shard_map/ppermute | solution.py:166

commit v5 on v3

--- a/solution.py
+++ b/solution.py
@@ -29,18 +29,12 @@
     partial_ref[...] = acc_ref[...].astype(jnp.bfloat16)
 
 
-def first_kernel(table_ref, panel_ref, own_ref, other_ref, partial_ref, acc_ref, held_ref, sems):
-    slots = own_ref.shape[0]
-    copies = [pltpu.make_async_copy(own_ref.at[slot], held_ref.at[slot], sems.at[slot]) for slot in range(slots)]
-    for copy in copies:
-        copy.start()
-
-    def held(slot):
-        copies[slot].wait()
-        return held_ref[slot]
-
-    groups = (NOTE, slots, lambda slot: other_ref[slot]), (0, slots, held)
-    add_tiles(table_ref, panel_ref, groups, partial_ref, acc_ref)
+def spread_kernel(core_ref, keep_ref, arrived_ref, own_ref, t0_ref, copies_ref):
+    core = core_ref[0]
+    t0_ref[core] = keep_ref[...]
+    t0_ref[1 - core] = arrived_ref[: keep_ref.shape[0]]
+    for group in range(copies_ref.shape[0]):
+        copies_ref[group] = t0_ref[...]
 
 
 def tile_kernel(table_ref, panel_ref, own_ref, other_ref, partial_ref, acc_ref):
@@ -94,22 +88,34 @@
         ]
     ).astype(jnp.bfloat16)
     send = jnp.concatenate([give, jnp.pad(note, ((0, half - NOTE), (0, TILE - slots)))])
+    send = lax.optimization_barrier(send)
     arrived = lax.ppermute(send, "c", SWAP)
-    field = ordered(keep, arrived[:half])
-    table = jnp.concatenate([note, arrived[half : half + NOTE, :slots]]).astype(jnp.int32)
-    field, table, slabs = lax.optimization_barrier((field, table, slabs))
+    notes = [both[half : half + NOTE, :slots] for both in (send, arrived)]
+    table = jnp.concatenate(notes).astype(jnp.int32)
+    params = pltpu.CompilerParams(vmem_limit_bytes=4 * 1024 * 1024)
+    groups = SIZES[1] * SIZES[0]
+    field, copies = pl.pallas_call(
+        spread_kernel,
+        out_shape=tuple(jax.ShapeDtypeStruct(more + (2, half, TILE), jnp.bfloat16) for more in ((), (groups,))),
+        in_specs=[SMEM, VMEM, VMEM, pl.BlockSpec(memory_space=pltpu.HBM)],
+        out_specs=(VMEM, VMEM),
+        compiler_params=params,
+        name="spread",
+    )(core.reshape(1), keep, arrived, pltpu.with_memory_space_constraint(slabs, pltpu.HBM))
+    copies, table, slabs = lax.optimization_barrier((copies, table, slabs))
     others = lax.ppermute(slabs, "c", SWAP)
 
     rows = SIZES[2] * SIZES[3] * SIZES[4]
     partial = jax.ShapeDtypeStruct((rows, half, TILE), jnp.bfloat16)
     plane = jax.ShapeDtypeStruct((2, half, TILE), jnp.float32)
     acc = pltpu.VMEM(partial.shape, jnp.float32)
-    params = pltpu.CompilerParams(vmem_limit_bytes=4 * 1024 * 1024)
+
+    def exchange(copies):
+        panel = lax.all_to_all(copies, ("zl", "x"), 0, 0, tiled=True)
+        return panel.reshape((SIZES[1], SIZES[0]) + copies.shape[1:])
 
     def gather(field_bf):
-        copies = jnp.broadcast_to(field_bf[None], (SIZES[1] * SIZES[0],) + field_bf.shape)
-        panel = lax.all_to_all(copies, ("zl", "x"), 0, 0, tiled=True)
-        return panel.reshape((SIZES[1], SIZES[0]) + field_bf.shape)
+        return exchange(jnp.broadcast_to(field_bf[None], (groups,) + field_bf.shape))
 
     def total(parts, axis):
         arrived = lax.all_to_all(parts, axis, 0, 0, tiled=True)
@@ -120,17 +126,6 @@
         along_y = total(part.reshape(SIZES[2], -1, half, TILE), "y").astype(jnp.bfloat16)
         return total(along_y.reshape(SIZES[3], 2, half, TILE), "zh")
 
-    t1 = reduce(
-        pl.pallas_call(
-            first_kernel,
-            out_shape=partial,
-            in_specs=[SMEM, VMEM, pl.BlockSpec(memory_space=pltpu.HBM), VMEM],
-            out_specs=VMEM,
-            scratch_shapes=[acc, pltpu.VMEM(slabs.shape, slabs.dtype), pltpu.SemaphoreType.DMA((slots,))],
-            compiler_params=pltpu.CompilerParams(vmem_limit_bytes=16 * 1024 * 1024),
-            name="first",
-        )(table, gather(field), pltpu.with_memory_space_constraint(slabs, pltpu.HBM), others)
-    )
     following = pl.pallas_call(
         tile_kernel,
         out_shape=partial,
@@ -140,6 +135,7 @@
         compiler_params=params,
         name="tiles",
     )
+    t1 = reduce(following(table, exchange(copies), slabs, others))
 
     def settled(value):
         return lax.optimization_barrier((value, value.astype(jnp.bfloat16)))

time: 221 us -> 220 us (level)
    pallas_call x1 -> x2, Pallas kernels: 5.25 us -> 3.26 us  [the longest x1 3.22 us: on_device(): t1 = reduce(following(table, exchange(copies), slabs, others))]
where the time goes in v5:
time: 220 us; the launch traced here: 219 us
  blocking collectives  174 us (79%)
  starting transfers between devices  26.2 us (12%)
  Pallas kernels  12.9 us (6%)
  other arithmetic  2.82 us (1%)
    all_to_all x8, blocking collectives, total(): arrived = lax.all_to_all(parts, axis, 0, 0, tiled=True)  108 us
    all_to_all x4, blocking collectives, exchange(): panel = lax.all_to_all(copies, ('zl', 'x'), 0, 0, tiled=True)  66 us
    ppermute x1, starting transfers between devices, on_device(): its = lax.ppermute(jnp.where(first, heat[1], heat[0]), 'c', SWAP)  15.2 us
    ppermute x1, starting transfers between devices, on_device(): arrived = lax.ppermute(send, 'c', SWAP)  8.78 us
  transfers between devices with their start and end apart: 3, of which 2 were waited for; matrix products, arithmetic and copies ran while one was open for 0% of the time, Pallas kernels for 0%

profile of v5, /device:TPU:1, one launch (start us, length us, event | category | flops | bytes accessed | tf_op | source)
XLA Modules:
  0.0 218.8 jit_solution(5394508168434309418)
XLA Ops:
  1.0 0.9 convert_bitcast_fusion
  1.9 0.7 broadcast_select_fusion
  2.7 8.8 %collective-permute-start = (bf16[32,512]{1,0:T(8,128)(2,1)S(1)}, bf16[32,512]{1,0:T(8,128)(2,1)S(1)}, u32[]{:S(2)}, u32[]{:S(2)}) collective-permute-start(bf16[32,512]{1,0:T(8,128)(2,1)S(1)} %fusion.2), channel_id=1, source_target_pairs={{0,1},{1,0},{2,3},{3,2},{4,5},{5,4},{6,7},{7,6},{8,9},{9,8},{10,11... | collective-permute-start | bytes 98312 | tf_op jit(solution)/shard_map/ppermute | solution.py:92
  11.5 0.8 collective-permute-done.arrived_ref
  12.4 2.3 %collective-permute-start.1 = (bf16[9,512,512]{2,1,0:T(8,128)(2,1)S(1)}, bf16[9,512,512]{2,1,0:T(8,128)(2,1)S(1)}, u32[]{:S(2)}, u32[]{:S(2)}) collective-permute-start(bf16[9,512,512]{2,1,0:T(8,128)(2,1)S(1)} %bitcast.40), channel_id=1, source_target_pairs={{0,1},{1,0},{2,3},{3,2},{4,5},{5,4},{6,7},{7,6},{8,9},{9,8},{10,11... | collective-permute-start | bytes 14155784 | tf_op jit(solution)/shard_map/ppermute | solution.py:106
  14.7 16.9 %all_to_all.60 = bf16[16,2,16,512]{3,2,1,0:T(8,128)(2,1)S(1)} all-to-all(bf16[16,2,16,512]{3,2,1,0:T(8,128)(2,1)S(1)} %get-tuple-element.21), channel_id=1, replica_groups=mesh['x'=4,'zl'=4,'y'=4,'zh'=4,'c'=2] {'zl','x'}, dimensions={0} | all-to-all | bytes 1048576 | tf_op jit(solution)/shard_map/all_to_all | solution.py:114
  31.6 3.2 %tiles.3 = bf16[32,16,512]{2,1,0:T(8,128)(2,1)S(1)} custom-call(s32[8,9]{1,0:T(8,128)S(1)} %maximum_convert_fusion.table_ref, bf16[4,4,2,16,512]{4,3,2,1,0:T(8,128)(2,1)S(1)} %bitcast.46, bf16[9,512,512]{2,1,0:T(8,128)(2,1)S(1)} %bitcast.41, bf16[9,512,512]{2,1,0:T(8,128)(2,1)S(1)} %collective-permute-done.1.other_ref), custom_call_target="tpu_custom_call" | custom-call | tf_op jit(solution)/shard_map/tiles/pallas_call | solution.py:138
  34.8 11.0 %all_to_all.61 = bf16[4,8,16,512]{3,2,1,0:T(8,128)(2,1)S(1)} all-to-all(bf16[4,8,16,512]{3,2,1,0:T(8,128)(2,1)S(1)} %bitcast.47), channel_id=1, replica_groups=mesh['x'=4,'zl'=4,'y'=4,'zh'=4,'c'=2] {'y'}, dimensions={0} | all-to-all | bytes 1048576 | tf_op jit(solution)/shard_map/all_to_all | solution.py:121
  45.9 24.2 %all_to_all.62 = bf16[4,2,16,512]{3,2,1,0:T(8,128)(2,1)S(1)} all-to-all(bf16[4,2,16,512]{3,2,1,0:T(8,128)(2,1)S(1)} %bitcast.53), channel_id=1, replica_groups=mesh['x'=4,'zl'=4,'y'=4,'zh'=4,'c'=2] {'zh'}, dimensions={0} | all-to-all | bytes 262144 | tf_op jit(solution)/shard_map/all_to_all | solution.py:121
  70.1 17.0 %all_to_all.63 = bf16[16,2,16,512]{3,2,1,0:T(8,128)(2,1)S(1)} all-to-all(bf16[16,2,16,512]{3,2,1,0:T(8,128)(2,1)S(1)} %broadcast_in_dim.15), channel_id=1, replica_groups=mesh['x'=4,'zl'=4,'y'=4,'zh'=4,'c'=2] {'zl','x'}, dimensions={0} | all-to-all | bytes 1048576 | tf_op jit(solution)/shard_map/all_to_all | solution.py:114
  87.2 3.2 %tiles.4 = bf16[32,16,512]{2,1,0:T(8,128)(2,1)S(1)} custom-call(s32[8,9]{1,0:T(8,128)S(1)} %maximum_convert_fusion.table_ref, bf16[4,4,2,16,512]{4,3,2,1,0:T(8,128)(2,1)S(1)} %bitcast.48, bf16[9,512,512]{2,1,0:T(8,128)(2,1)S(1)} %bitcast.42, bf16[9,512,512]{2,1,0:T(8,128)(2,1)S(1)} %collective-permute-done.1.other_ref), custom_call_target="tpu_custom_call" | custom-call | tf_op jit(solution)/shard_map/tiles/pallas_call | solution.py:144
  90.4 9.3 %all_to_all.64 = bf16[4,8,16,512]{3,2,1,0:T(8,128)(2,1)S(1)} all-to-all(bf16[4,8,16,512]{3,2,1,0:T(8,128)(2,1)S(1)} %bitcast.49), channel_id=1, replica_groups=mesh['x'=4,'zl'=4,'y'=4,'zh'=4,'c'=2] {'y'}, dimensions={0} | all-to-all | bytes 1048576 | tf_op jit(solution)/shard_map/all_to_all | solution.py:121
  99.8 15.8 %all_to_all.65 = bf16[4,2,16,512]{3,2,1,0:T(8,128)(2,1)S(1)} all-to-all(bf16[4,2,16,512]{3,2,1,0:T(8,128)(2,1)S(1)} %bitcast.54), channel_id=1, replica_groups=mesh['x'=4,'zl'=4,'y'=4,'zh'=4,'c'=2] {'zh'}, dimensions={0} | all-to-all | bytes 262144 | tf_op jit(solution)/shard_map/all_to_all | solution.py:121
  115.7 17.4 %all_to_all.66 = bf16[16,2,16,512]{3,2,1,0:T(8,128)(2,1)S(1)} all-to-all(bf16[16,2,16,512]{3,2,1,0:T(8,128)(2,1)S(1)} %broadcast_in_dim.32), channel_id=1, replica_groups=mesh['x'=4,'zl'=4,'y'=4,'zh'=4,'c'=2] {'zl','x'}, dimensions={0} | all-to-all | bytes 1048576 | tf_op jit(solution)/shard_map/all_to_all | solution.py:114
  133.2 3.2 %tiles.5 = bf16[32,16,512]{2,1,0:T(8,128)(2,1)S(1)} custom-call(s32[8,9]{1,0:T(8,128)S(1)} %maximum_convert_fusion.table_ref, bf16[4,4,2,16,512]{4,3,2,1,0:T(8,128)(2,1)S(1)} %bitcast.50, bf16[9,512,512]{2,1,0:T(8,128)(2,1)S(1)} %bitcast.43, bf16[9,512,512]{2,1,0:T(8,128)(2,1)S(1)} %collective-permute-done.1.other_ref), custom_call_target="tpu_custom_call" | custom-call | tf_op jit(solution)/shard_map/tiles/pallas_call | solution.py:146
  136.4 9.3 %all_to_all.67 = bf16[4,8,16,512]{3,2,1,0:T(8,128)(2,1)S(1)} all-to-all(bf16[4,8,16,512]{3,2,1,0:T(8,128)(2,1)S(1)} %bitcast.51), channel_id=1, replica_groups=mesh['x'=4,'zl'=4,'y'=4,'zh'=4,'c'=2] {'y'}, dimensions={0} | all-to-all | bytes 1048576 | tf_op jit(solution)/shard_map/all_to_all | solution.py:121
  145.8 14.4 %all_to_all.68 = bf16[4,2,16,512]{3,2,1,0:T(8,128)(2,1)S(1)} all-to-all(bf16[4,2,16,512]{3,2,1,0:T(8,128)(2,1)S(1)} %bitcast.55), channel_id=1, replica_groups=mesh['x'=4,'zl'=4,'y'=4,'zh'=4,'c'=2] {'zh'}, dimensions={0} | all-to-all | bytes 262144 | tf_op jit(solution)/shard_map/all_to_all | solution.py:121
  160.3 14.5 %all_to_all.69 = bf16[16,2,16,512]{3,2,1,0:T(8,128)(2,1)S(1)} all-to-all(bf16[16,2,16,512]{3,2,1,0:T(8,128)(2,1)S(1)} %broadcast_in_dim.33), channel_id=1, replica_groups=mesh['x'=4,'zl'=4,'y'=4,'zh'=4,'c'=2] {'zl','x'}, dimensions={0} | all-to-all | bytes 1048576 | tf_op jit(solution)/shard_map/all_to_all | solution.py:114
  174.9 3.2 %last.1 = (bf16[32,16,512]{2,1,0:T(8,128)(2,1)S(1)}, f32[2,16,512]{2,1,0:T(8,128)S(1)}, f32[2,16,512]{2,1,0:T(8,128)S(1)}) custom-call(s32[8,9]{1,0:T(8,128)S(1)} %maximum_convert_fusion.table_ref, f32[5]{0:T(128)S(1)} %copy-done.1, bf16[4,4,2,16,512]{4,3,2,1,0:T(8,128)(2,1)S(1)} %bitcast.45, bf16[9,512,512]{2,1,0:T(8,128)(2,1)S(1)} %bitcast.44, ...), custom_call_target="tpu_custom_call" | custom-call | tf_op jit(solution)/shard_map/last/pallas_call | solution.py:149
  178.1 9.3 %all_to_all.70 = bf16[4,8,16,512]{3,2,1,0:T(8,128)(2,1)S(1)} all-to-all(bf16[4,8,16,512]{3,2,1,0:T(8,128)(2,1)S(1)} %bitcast.52), channel_id=1, replica_groups=mesh['x'=4,'zl'=4,'y'=4,'zh'=4,'c'=2] {'y'}, dimensions={0} | all-to-all | bytes 1048576 | tf_op jit(solution)/shard_map/all_to_all | solution.py:121
  187.5 14.6 %all_to_all.71 = bf16[4,2,16,512]{3,2,1,0:T(8,128)(2,1)S(1)} all-to-all(bf16[4,2,16,512]{3,2,1,0:T(8,128)(2,1)S(1)} %bitcast.56), channel_id=1, replica_groups=mesh['x'=4,'zl'=4,'y'=4,'zh'=4,'c'=2] {'zh'}, dimensions={0} | all-to-all | bytes 262144 | tf_op jit(solution)/shard_map/all_to_all | solution.py:121
  202.2 15.2 %collective-permute-start.2 = (f32[16,512]{1,0:T(8,128)S(1)}, f32[16,512]{1,0:T(8,128)S(1)}, u32[]{:S(2)}, u32[]{:S(2)}) collective-permute-start(f32[16,512]{1,0:T(8,128)S(1)} %get-tuple-element.40), channel_id=1, source_target_pairs={{0,1},{1,0},{2,3},{3,2},{4,5},{5,4},{6,7},{7,6},{8,9},{9,8},{10,11... | collective-permute-start | bytes 98312 | tf_op jit(solution)/shard_map/ppermute | solution.py:161
  217.4 0.8 collective-permute-done.2
  218.2 0.6 maximum_select_fusion
  (25 shorter events, 0.9 us)
Async XLA Ops:
  0.0 12.4 %copy-start = (bf16[1,1,9,512,512]{4,3,2,1,0:T(8,128)(2,1)S(1)}, bf16[1,1,9,512,512]{4,3,2,1,0:T(8,128)(2,1)}, u32[]{:S(2)}) copy-start(bf16[1,1,9,512,512]{4,3,2,1,0:T(8,128)(2,1)} %param.6) | copy-start | bytes 14155780
  2.7 9.6 %collective-permute-start = (bf16[32,512]{1,0:T(8,128)(2,1)S(1)}, bf16[32,512]{1,0:T(8,128)(2,1)S(1)}, u32[]{:S(2)}, u32[]{:S(2)}) collective-permute-start(bf16[32,512]{1,0:T(8,128)(2,1)S(1)} %fusion.2), channel_id=1, source_target_pairs={{0,1},{1,0},{2,3},{3,2},{4,5},{5,4},{6,7},{7,6},{8,9},{9,8},{10,11... | collective-permute-start | bytes 98312 | tf_op jit(solution)/shard_map/ppermute | solution.py:92
  12.4 19.2 %collective-permute-start.1 = (bf16[9,512,512]{2,1,0:T(8,128)(2,1)S(1)}, bf16[9,512,512]{2,1,0:T(8,128)(2,1)S(1)}, u32[]{:S(2)}, u32[]{:S(2)}) collective-permute-start(bf16[9,512,512]{2,1,0:T(8,128)(2,1)S(1)} %bitcast.40), channel_id=1, source_target_pairs={{0,1},{1,0},{2,3},{3,2},{4,5},{5,4},{6,7},{7,6},{8,9},{9,8},{10,11... | collective-permute-start | bytes 14155784 | tf_op jit(solution)/shard_map/ppermute | solution.py:106
  133.2 41.7 %copy-start.1 = (f32[5]{0:T(128)S(1)}, f32[5]{0:T(128)}, u32[]{:S(2)}) copy-start(f32[5]{0:T(128)} %weight_ref.1) | copy-start | bytes 64
  202.2 16.0 %collective-permute-start.2 = (f32[16,512]{1,0:T(8,128)S(1)}, f32[16,512]{1,0:T(8,128)S(1)}, u32[]{:S(2)}, u32[]{:S(2)}) collective-permute-start(f32[16,512]{1,0:T(8,128)S(1)} %get-tuple-element.40), channel_id=1, source_target_pairs={{0,1},{1,0},{2,3},{3,2},{4,5},{5,4},{6,7},{7,6},{8,9},{9,8},{10,11... | collective-permute-start | bytes 98312 | tf_op jit(solution)/shard_map/ppermute | solution.py:161

commit v6 on v5

--- a/solution.py
+++ b/solution.py
@@ -14,33 +14,56 @@
 ROW, COL, COUNT, CORE, NOTE = 0, 1, 2, 3, 4
 
 
-def add_tiles(table_ref, panel_ref, groups, partial_ref, acc_ref):
+def first_kernel(index_ref, count_ref, core_ref, probes_ref, panel_ref, own_ref, mine_ref, theirs_ref, acc_ref):
     acc_ref[...] = jnp.zeros_like(acc_ref)
-    for note, slots, tile_of in groups:
+    slots = own_ref.shape[0]
+    count, core = count_ref[0], core_ref[0]
+    for slot in range(slots):
+        row, col = index_ref[ROW, slot], index_ref[COL, slot]
+        picked = panel_ref[col % SIZES[1], col // SIZES[1]]
+        picked = jnp.where(slot < count, picked, jnp.zeros_like(picked))
+        acc_ref[row] += lax.dot_general(
+            picked, own_ref[slot], (((1,), (1,)), ((), ())), preferred_element_type=jnp.float32
+        )
+    rows, half = acc_ref.shape[0], mine_ref.shape[1]
+    for out_ref, which in ((mine_ref, core), (theirs_ref, 1 - core)):
+        columns = pl.ds(pl.multiple_of(which * half, half), half)
+        out_ref[:rows] = acc_ref[:, columns].astype(jnp.bfloat16)
+        out_ref[rows] = probes_ref[columns]
+    shape = (half, 128)
+    line, lane = lax.broadcasted_iota(jnp.int32, shape, 0), lax.broadcasted_iota(jnp.int32, shape, 1)
+    note = jnp.where(line == COUNT, count, jnp.where(line == CORE, core, 0))
+    for slot in range(slots):
+        place = jnp.where(line == ROW, index_ref[ROW, slot], index_ref[COL, slot])
+        note = jnp.where((lane == slot) & (line <= COL), place, note)
+    theirs_ref[rows + 1] = jnp.zeros(theirs_ref.shape[1:], jnp.bfloat16)
+    theirs_ref[rows + 1, :, :128] = note.astype(jnp.float32).astype(jnp.bfloat16)
+
+
+def spread_kernel(probes_hbm, index_hbm, own_ref, copies_ref, kept_ref, index_ref, sems):
+    fetch_probes = pltpu.make_async_copy(probes_hbm, kept_ref, sems.at[0])
+    fetch_index = pltpu.make_async_copy(index_hbm, index_ref, sems.at[1])
+    fetch_probes.start()
+    fetch_index.start()
+    fetch_probes.wait()
+    for group in range(copies_ref.shape[0]):
+        copies_ref[group] = kept_ref[...]
+    fetch_index.wait()
+
+
+def tile_kernel(table_ref, panel_ref, own_ref, other_ref, partial_ref, acc_ref):
+    acc_ref[...] = jnp.zeros_like(acc_ref)
+    for tiles_ref, note in ((own_ref, 0), (other_ref, NOTE)):
         parity = table_ref[note + CORE, 0]
-        for slot in range(slots):
+        for slot in range(own_ref.shape[0]):
             row = table_ref[note + ROW, slot]
             col = table_ref[note + COL, slot]
             picked = panel_ref[col % SIZES[1], col // SIZES[1], parity]
             picked = jnp.where(slot < table_ref[note + COUNT, 0], picked, jnp.zeros_like(picked))
             acc_ref[row] += lax.dot_general(
-                picked, tile_of(slot), (((1,), (1,)), ((), ())), preferred_element_type=jnp.float32
+                picked, tiles_ref[slot], (((1,), (1,)), ((), ())), preferred_element_type=jnp.float32
             )
     partial_ref[...] = acc_ref[...].astype(jnp.bfloat16)
-
-
-def spread_kernel(core_ref, keep_ref, arrived_ref, own_ref, t0_ref, copies_ref):
-    core = core_ref[0]
-    t0_ref[core] = keep_ref[...]
-    t0_ref[1 - core] = arrived_ref[: keep_ref.shape[0]]
-    for group in range(copies_ref.shape[0]):
-        copies_ref[group] = t0_ref[...]
-
-
-def tile_kernel(table_ref, panel_ref, own_ref, other_ref, partial_ref, acc_ref):
-    slots = own_ref.shape[0]
-    groups = (NOTE, slots, lambda slot: other_ref[slot]), (0, slots, lambda slot: own_ref[slot])
-    add_tiles(table_ref, panel_ref, groups, partial_ref, acc_ref)
 
 
 def last_kernel(
@@ -71,39 +94,31 @@
 def on_device(probes, tiles, tile_index, tile_count, coefficients):
     slabs = tiles[0, 0]
     half = probes.shape[0] // 2
+    slots = slabs.shape[0]
     core = lax.axis_index("c").astype(jnp.int32)
     first = core == 0
+    index = tile_index[0, 0].T
+    count = jnp.minimum(tile_count[0], slots)
+    core, first, count = lax.optimization_barrier((core, first, count))
+    params = pltpu.CompilerParams(vmem_limit_bytes=4 * 1024 * 1024)
+    groups = SIZES[1] * SIZES[0]
+    copies, probes, index = pl.pallas_call(
+        spread_kernel,
+        out_shape=(
+            jax.ShapeDtypeStruct((groups,) + probes.shape, probes.dtype),
+            jax.ShapeDtypeStruct(probes.shape, probes.dtype),
+            jax.ShapeDtypeStruct(index.shape, index.dtype),
+        ),
+        in_specs=[pl.BlockSpec(memory_space=pltpu.HBM)] * 3,
+        out_specs=(VMEM, VMEM, VMEM),
+        scratch_shapes=[pltpu.SemaphoreType.DMA((2,))],
+        compiler_params=params,
+        name="spread",
+    )(*(pltpu.with_memory_space_constraint(value, pltpu.HBM) for value in (probes, index, slabs)))
+    copies, core, count = lax.optimization_barrier((copies, core, count))
 
     def ordered(mine, its):
         return jnp.where(first, jnp.stack([mine, its]), jnp.stack([its, mine]))
-
-    keep = jnp.where(first, probes[:half], probes[half:])
-    give = jnp.where(first, probes[half:], probes[:half])
-    slots = slabs.shape[0]
-    note = jnp.concatenate(
-        [
-            tile_index[0, 0].T,
-            jnp.broadcast_to(tile_count, (1, slots)),
-            jnp.broadcast_to(core, (1, slots)),
-        ]
-    ).astype(jnp.bfloat16)
-    send = jnp.concatenate([give, jnp.pad(note, ((0, half - NOTE), (0, TILE - slots)))])
-    send = lax.optimization_barrier(send)
-    arrived = lax.ppermute(send, "c", SWAP)
-    notes = [both[half : half + NOTE, :slots] for both in (send, arrived)]
-    table = jnp.concatenate(notes).astype(jnp.int32)
-    params = pltpu.CompilerParams(vmem_limit_bytes=4 * 1024 * 1024)
-    groups = SIZES[1] * SIZES[0]
-    field, copies = pl.pallas_call(
-        spread_kernel,
-        out_shape=tuple(jax.ShapeDtypeStruct(more + (2, half, TILE), jnp.bfloat16) for more in ((), (groups,))),
-        in_specs=[SMEM, VMEM, VMEM, pl.BlockSpec(memory_space=pltpu.HBM)],
-        out_specs=(VMEM, VMEM),
-        compiler_params=params,
-        name="spread",
-    )(core.reshape(1), keep, arrived, pltpu.with_memory_space_constraint(slabs, pltpu.HBM))
-    copies, table, slabs = lax.optimization_barrier((copies, table, slabs))
-    others = lax.ppermute(slabs, "c", SWAP)
 
     rows = SIZES[2] * SIZES[3] * SIZES[4]
     partial = jax.ShapeDtypeStruct((rows, half, TILE), jnp.bfloat16)
@@ -126,6 +141,22 @@
         along_y = total(part.reshape(SIZES[2], -1, half, TILE), "y").astype(jnp.bfloat16)
         return total(along_y.reshape(SIZES[3], 2, half, TILE), "zh")
 
+    mine, theirs = pl.pallas_call(
+        first_kernel,
+        out_shape=tuple(jax.ShapeDtypeStruct((rows + more, half, TILE), jnp.bfloat16) for more in (1, 2)),
+        in_specs=[SMEM, SMEM, SMEM, VMEM, VMEM, VMEM],
+        out_specs=(VMEM, VMEM),
+        scratch_shapes=[pltpu.VMEM((rows, 2 * half, TILE), jnp.float32)],
+        compiler_params=params,
+        name="first",
+    )(index, count, core.reshape(1), probes, exchange(copies), slabs)
+    arrived = lax.ppermute(theirs, "c", SWAP)
+    part = (mine[:rows].astype(jnp.float32) + arrived[:rows].astype(jnp.float32)).astype(jnp.bfloat16)
+    field = ordered(mine[rows], arrived[rows])
+    table = jnp.concatenate([both[rows + 1, :NOTE, :slots] for both in (theirs, arrived)]).astype(jnp.int32)
+    part, field, table, slabs = lax.optimization_barrier((part, field, table, slabs))
+    others = lax.ppermute(slabs, "c", SWAP)
+    t1 = reduce(part)
     following = pl.pallas_call(
         tile_kernel,
         out_shape=partial,
@@ -135,7 +166,6 @@
         compiler_params=params,
         name="tiles",
     )
-    t1 = reduce(following(table, exchange(copies), slabs, others))
 
     def settled(value):
         return lax.optimization_barrier((value, value.astype(jnp.bfloat16)))

time: 220 us -> 221 us (level)
  blocking collectives: 174 us -> 181 us
  starting transfers between devices: 26.2 us -> 21.9 us
    ppermute x1, starting transfers between devices: 8.78 us -> 4.54 us  [on_device(): arrived = lax.ppermute(theirs, 'c', SWAP)]
    all_to_all x8, blocking collectives: 108 us -> 112 us  [total(): arrived = lax.all_to_all(parts, axis, 0, 0, tiled=True)]
    all_to_all x4, blocking collectives: 66 us -> 69.3 us  [exchange(): panel = lax.all_to_all(copies, ('zl', 'x'), 0, 0, tiled=True)]
where the time goes in v6:
time: 221 us
  blocking collectives  181 us (82%)
  starting transfers between devices  21.9 us (10%)
  Pallas kernels  12.7 us (6%)
  waiting for transfers between devices  2.38 us (1%)
    all_to_all x8, blocking collectives, total(): arrived = lax.all_to_all(parts, axis, 0, 0, tiled=True)  112 us
    all_to_all x4, blocking collectives, exchange(): panel = lax.all_to_all(copies, ('zl', 'x'), 0, 0, tiled=True)  69.3 us
    ppermute x1, starting transfers between devices, on_device(): its = lax.ppermute(jnp.where(first, heat[1], heat[0]), 'c', SWAP)  15.1 us
    ppermute x1, starting transfers between devices, on_device(): arrived = lax.ppermute(theirs, 'c', SWAP)  4.54 us
  transfers between devices with their start and end apart: 3, of which 2 were waited for; matrix products, arithmetic and copies ran while one was open for 0% of the time, Pallas kernels for 0%

profile of v6, /device:TPU:1, one launch (start us, length us, event | category | flops | bytes accessed | tf_op | source)
XLA Modules:
  0.0 220.7 jit_solution(15742191939457277194)
XLA Ops:
  0.7 1.0 spread.1
  1.6 22.7 %all_to_all.60 = bf16[16,32,512]{2,1,0:T(8,128)(2,1)S(1)} all-to-all(bf16[16,32,512]{2,1,0:T(8,128)(2,1)S(1)} %get-tuple-element.37), channel_id=1, replica_groups=mesh['x'=4,'zl'=4,'y'=4,'zh'=4,'c'=2] {'zl','x'}, dimensions={0} | all-to-all | bytes 1048576 | tf_op jit(solution)/shard_map/all_to_all | solution.py:129
  24.4 2.1 first.1
  26.4 4.5 %collective-permute-start = (bf16[34,16,512]{2,1,0:T(8,128)(2,1)S(1)}, bf16[34,16,512]{2,1,0:T(8,128)(2,1)S(1)}, u32[]{:S(2)}, u32[]{:S(2)}) collective-permute-start(bf16[34,16,512]{2,1,0:T(8,128)(2,1)S(1)} %get-tuple-element.39), channel_id=1, source_target_pairs={{0,1},{1,0},{2,3},{3,2},{4,5},{5,4},{6,7},{7,6},{8,9},{9,8},{10,11... | collective-permute-start | bytes 1671176 | tf_op jit(solution)/shard_map/ppermute | solution.py:153
  31.0 1.5 collective-permute-done
  32.6 0.2 add_convert_fusion
  32.8 2.3 %collective-permute-start.1 = (bf16[9,512,512]{2,1,0:T(8,128)(2,1)S(1)}, bf16[9,512,512]{2,1,0:T(8,128)(2,1)S(1)}, u32[]{:S(2)}, u32[]{:S(2)}) collective-permute-start(bf16[9,512,512]{2,1,0:T(8,128)(2,1)S(1)} %bitcast.41), channel_id=1, source_target_pairs={{0,1},{1,0},{2,3},{3,2},{4,5},{5,4},{6,7},{7,6},{8,9},{9,8},{10,11... | collective-permute-start | bytes 14155784 | tf_op jit(solution)/shard_map/ppermute | solution.py:158
  35.1 13.1 %all_to_all.61 = bf16[4,8,16,512]{3,2,1,0:T(8,128)(2,1)S(1)} all-to-all(bf16[4,8,16,512]{3,2,1,0:T(8,128)(2,1)S(1)} %bitcast.52), channel_id=1, replica_groups=mesh['x'=4,'zl'=4,'y'=4,'zh'=4,'c'=2] {'y'}, dimensions={0} | all-to-all | bytes 1048576 | tf_op jit(solution)/shard_map/all_to_all | solution.py:136
  48.3 24.3 %all_to_all.62 = bf16[4,2,16,512]{3,2,1,0:T(8,128)(2,1)S(1)} all-to-all(bf16[4,2,16,512]{3,2,1,0:T(8,128)(2,1)S(1)} %bitcast.53), channel_id=1, replica_groups=mesh['x'=4,'zl'=4,'y'=4,'zh'=4,'c'=2] {'zh'}, dimensions={0} | all-to-all | bytes 262144 | tf_op jit(solution)/shard_map/all_to_all | solution.py:136
  72.6 15.3 %all_to_all.63 = bf16[16,2,16,512]{3,2,1,0:T(8,128)(2,1)S(1)} all-to-all(bf16[16,2,16,512]{3,2,1,0:T(8,128)(2,1)S(1)} %broadcast_in_dim.6), channel_id=1, replica_groups=mesh['x'=4,'zl'=4,'y'=4,'zh'=4,'c'=2] {'zl','x'}, dimensions={0} | all-to-all | bytes 1048576 | tf_op jit(solution)/shard_map/all_to_all | solution.py:129
  87.9 3.2 %tiles.2 = bf16[32,16,512]{2,1,0:T(8,128)(2,1)S(1)} custom-call(s32[8,9]{1,0:T(8,128)S(1)} %maximum_convert_fusion.table_ref, bf16[4,4,2,16,512]{4,3,2,1,0:T(8,128)(2,1)S(1)} %bitcast.47, bf16[9,512,512]{2,1,0:T(8,128)(2,1)S(1)} %bitcast.42, bf16[9,512,512]{2,1,0:T(8,128)(2,1)S(1)} %collective-permute-done.1.other_ref), custom_call_target="tpu_custom_call" | custom-call | tf_op jit(solution)/shard_map/tiles/pallas_call | solution.py:174
  91.2 9.3 %all_to_all.64 = bf16[4,8,16,512]{3,2,1,0:T(8,128)(2,1)S(1)} all-to-all(bf16[4,8,16,512]{3,2,1,0:T(8,128)(2,1)S(1)} %bitcast.48), channel_id=1, replica_groups=mesh['x'=4,'zl'=4,'y'=4,'zh'=4,'c'=2] {'y'}, dimensions={0} | all-to-all | bytes 1048576 | tf_op jit(solution)/shard_map/all_to_all | solution.py:136
  100.6 17.7 %all_to_all.65 = bf16[4,2,16,512]{3,2,1,0:T(8,128)(2,1)S(1)} all-to-all(bf16[4,2,16,512]{3,2,1,0:T(8,128)(2,1)S(1)} %bitcast.54), channel_id=1, replica_groups=mesh['x'=4,'zl'=4,'y'=4,'zh'=4,'c'=2] {'zh'}, dimensions={0} | all-to-all | bytes 262144 | tf_op jit(solution)/shard_map/all_to_all | solution.py:136
  118.3 16.6 %all_to_all.66 = bf16[16,2,16,512]{3,2,1,0:T(8,128)(2,1)S(1)} all-to-all(bf16[16,2,16,512]{3,2,1,0:T(8,128)(2,1)S(1)} %broadcast_in_dim.7), channel_id=1, replica_groups=mesh['x'=4,'zl'=4,'y'=4,'zh'=4,'c'=2] {'zl','x'}, dimensions={0} | all-to-all | bytes 1048576 | tf_op jit(solution)/shard_map/all_to_all | solution.py:129
  134.9 3.2 %tiles.3 = bf16[32,16,512]{2,1,0:T(8,128)(2,1)S(1)} custom-call(s32[8,9]{1,0:T(8,128)S(1)} %maximum_convert_fusion.table_ref, bf16[4,4,2,16,512]{4,3,2,1,0:T(8,128)(2,1)S(1)} %bitcast.49, bf16[9,512,512]{2,1,0:T(8,128)(2,1)S(1)} %bitcast.43, bf16[9,512,512]{2,1,0:T(8,128)(2,1)S(1)} %collective-permute-done.1.other_ref), custom_call_target="tpu_custom_call" | custom-call | tf_op jit(solution)/shard_map/tiles/pallas_call | solution.py:176
  138.1 9.3 %all_to_all.67 = bf16[4,8,16,512]{3,2,1,0:T(8,128)(2,1)S(1)} all-to-all(bf16[4,8,16,512]{3,2,1,0:T(8,128)(2,1)S(1)} %bitcast.50), channel_id=1, replica_groups=mesh['x'=4,'zl'=4,'y'=4,'zh'=4,'c'=2] {'y'}, dimensions={0} | all-to-all | bytes 1048576 | tf_op jit(solution)/shard_map/all_to_all | solution.py:136
  147.5 14.4 %all_to_all.68 = bf16[4,2,16,512]{3,2,1,0:T(8,128)(2,1)S(1)} all-to-all(bf16[4,2,16,512]{3,2,1,0:T(8,128)(2,1)S(1)} %bitcast.55), channel_id=1, replica_groups=mesh['x'=4,'zl'=4,'y'=4,'zh'=4,'c'=2] {'zh'}, dimensions={0} | all-to-all | bytes 262144 | tf_op jit(solution)/shard_map/all_to_all | solution.py:136
  162.0 14.7 %all_to_all.69 = bf16[16,2,16,512]{3,2,1,0:T(8,128)(2,1)S(1)} all-to-all(bf16[16,2,16,512]{3,2,1,0:T(8,128)(2,1)S(1)} %broadcast_in_dim.8), channel_id=1, replica_groups=mesh['x'=4,'zl'=4,'y'=4,'zh'=4,'c'=2] {'zl','x'}, dimensions={0} | all-to-all | bytes 1048576 | tf_op jit(solution)/shard_map/all_to_all | solution.py:129
  176.7 3.2 %last.1 = (bf16[32,16,512]{2,1,0:T(8,128)(2,1)S(1)}, f32[2,16,512]{2,1,0:T(8,128)S(1)}, f32[2,16,512]{2,1,0:T(8,128)S(1)}) custom-call(s32[8,9]{1,0:T(8,128)S(1)} %maximum_convert_fusion.table_ref, f32[5]{0:T(128)S(1)} %copy-done.1, bf16[4,4,2,16,512]{4,3,2,1,0:T(8,128)(2,1)S(1)} %bitcast.45, bf16[9,512,512]{2,1,0:T(8,128)(2,1)S(1)} %bitcast.44, ...), custom_call_target="tpu_custom_call" | custom-call | tf_op jit(solution)/shard_map/last/pallas_call | solution.py:179
  180.0 9.3 %all_to_all.70 = bf16[4,8,16,512]{3,2,1,0:T(8,128)(2,1)S(1)} all-to-all(bf16[4,8,16,512]{3,2,1,0:T(8,128)(2,1)S(1)} %bitcast.51), channel_id=1, replica_groups=mesh['x'=4,'zl'=4,'y'=4,'zh'=4,'c'=2] {'y'}, dimensions={0} | all-to-all | bytes 1048576 | tf_op jit(solution)/shard_map/all_to_all | solution.py:136
  189.4 14.6 %all_to_all.71 = bf16[4,2,16,512]{3,2,1,0:T(8,128)(2,1)S(1)} all-to-all(bf16[4,2,16,512]{3,2,1,0:T(8,128)(2,1)S(1)} %bitcast.56), channel_id=1, replica_groups=mesh['x'=4,'zl'=4,'y'=4,'zh'=4,'c'=2] {'zh'}, dimensions={0} | all-to-all | bytes 262144 | tf_op jit(solution)/shard_map/all_to_all | solution.py:136
  204.1 15.1 %collective-permute-start.2 = (f32[16,512]{1,0:T(8,128)S(1)}, f32[16,512]{1,0:T(8,128)S(1)}, u32[]{:S(2)}, u32[]{:S(2)}) collective-permute-start(f32[16,512]{1,0:T(8,128)S(1)} %get-tuple-element.60), channel_id=1, source_target_pairs={{0,1},{1,0},{2,3},{3,2},{4,5},{5,4},{6,7},{7,6},{8,9},{9,8},{10,11... | collective-permute-start | bytes 98312 | tf_op jit(solution)/shard_map/ppermute | solution.py:191
  219.2 0.8 collective-permute-done.2
  220.0 0.6 maximum_select_fusion
  (23 shorter events, 0.6 us)
Async XLA Ops:
  0.7 23.7 %copy-start = (bf16[1,1,9,512,512]{4,3,2,1,0:T(8,128)(2,1)S(1)}, bf16[1,1,9,512,512]{4,3,2,1,0:T(8,128)(2,1)}, u32[]{:S(2)}) copy-start(bf16[1,1,9,512,512]{4,3,2,1,0:T(8,128)(2,1)} %param.6) | copy-start | bytes 14155780
  26.4 6.1 %collective-permute-start = (bf16[34,16,512]{2,1,0:T(8,128)(2,1)S(1)}, bf16[34,16,512]{2,1,0:T(8,128)(2,1)S(1)}, u32[]{:S(2)}, u32[]{:S(2)}) collective-permute-start(bf16[34,16,512]{2,1,0:T(8,128)(2,1)S(1)} %get-tuple-element.39), channel_id=1, source_target_pairs={{0,1},{1,0},{2,3},{3,2},{4,5},{5,4},{6,7},{7,6},{8,9},{9,8},{10,11... | collective-permute-start | bytes 1671176 | tf_op jit(solution)/shard_map/ppermute | solution.py:153
  32.8 55.2 %collective-permute-start.1 = (bf16[9,512,512]{2,1,0:T(8,128)(2,1)S(1)}, bf16[9,512,512]{2,1,0:T(8,128)(2,1)S(1)}, u32[]{:S(2)}, u32[]{:S(2)}) collective-permute-start(bf16[9,512,512]{2,1,0:T(8,128)(2,1)S(1)} %bitcast.41), channel_id=1, source_target_pairs={{0,1},{1,0},{2,3},{3,2},{4,5},{5,4},{6,7},{7,6},{8,9},{9,8},{10,11... | collective-permute-start | bytes 14155784 | tf_op jit(solution)/shard_map/ppermute | solution.py:158
  134.9 41.8 %copy-start.1 = (f32[5]{0:T(128)S(1)}, f32[5]{0:T(128)}, u32[]{:S(2)}) copy-start(f32[5]{0:T(128)} %weight_ref.1) | copy-start | bytes 64
  204.1 16.0 %collective-permute-start.2 = (f32[16,512]{1,0:T(8,128)S(1)}, f32[16,512]{1,0:T(8,128)S(1)}, u32[]{:S(2)}, u32[]{:S(2)}) collective-permute-start(f32[16,512]{1,0:T(8,128)S(1)} %get-tuple-element.60), channel_id=1, source_target_pairs={{0,1},{1,0},{2,3},{3,2},{4,5},{5,4},{6,7},{7,6},{8,9},{9,8},{10,11... | collective-permute-start | bytes 98312 | tf_op jit(solution)/shard_map/ppermute | solution.py:191
